TPU v7x, 256 devices: a whole 4x4x8 slice. The times are simulated.
256 devices in a mesh: rows: 64 (over z, x, core), cols: 4 (over y).
Axes of the slice: x: 4, y: 4, z: 8, core: 2. Of those that a mesh axis runs over, the one named last changes fastest.
Arguments:
- front_rows: bfloat16 [8, 8192, 4096], P(None, 'rows', 'cols'), may hold values from -0.0625 to 0.0625
- heights: int32 [64, 8], P('rows'), may hold values from 1 to 128
- child_rows: bfloat16 [65536, 4096], P('rows', 'cols'), may hold values from -0.0625 to 0.0625
- child_dest: int32 [65536, 1], P('rows'), may hold values from 0 to 63; in each aligned block of 1024 rows (0 to 1023, 1024 to 2047, ...) at most 32 rows name the same one
- child_slot: int32 [65536], P('rows'), may hold values from 0 to 127
- parent_ids: int32 [1024], P('rows'), may hold values from 0 to 7
Outputs:
- r_rows: float32 [8, 128, 4096], P(None, None, ('cols', 'rows'))
Inputs may be any that keep to these rules, and one draw needn't show every extreme that they name: `child_dest`: in the rows of one device, at most 32 child rows name one index of rows.
All inputs are finite; a program needn't handle non-finite values.
Results may differ from a plain program's by a relative error of at most 0.002.
Values may be sent and summed in bfloat16 or wider, within the bound.
No kernel may reach another device: no remote copies, remote signals or barrier semaphores. Data moves between devices by JAX's collectives and lax.ppermute only.
A program may use at most 64 MiB of HBM per device.

v0:
```python
import jax
import jax.numpy as jnp
from jax import lax
from jax.sharding import PartitionSpec as P

NB = 128


def from_root(block, axis, holder):
    block = jnp.where(lax.axis_index(axis) == holder, block, jnp.zeros_like(block))
    return lax.psum(block, axis)


def solve_block(lower, columns):
    return jax.scipy.linalg.solve_triangular(lower, columns, lower=True)


def on_device(front_rows, heights, child_rows, child_dest, child_slot, parent_ids):
    fronts, height_cap, width = front_rows.shape
    peers = lax.axis_size("rows")
    child_count = child_rows.shape[0]
    capacity = max(2, 2 * child_count // peers)
    slots = peers * capacity
    destination = child_dest[:, 0]
    hits = (destination[:, None] == jnp.arange(peers, dtype=jnp.int32)[None, :]).astype(jnp.int32)
    before = jnp.cumsum(hits, axis=0) - hits
    position = jnp.sum(before * hits, axis=1)
    send_index = destination * capacity + position
    block_rows = child_count // parent_ids.shape[0]
    child_front = jnp.repeat(parent_ids, block_rows)
    send_rows = jnp.zeros((slots, width), jnp.bfloat16).at[send_index].set(child_rows)
    send_owner = jnp.zeros((slots,), jnp.int32).at[send_index].set(child_front)
    send_front = send_owner.astype(jnp.bfloat16)
    send_slot = (
        jnp.zeros((slots,), jnp.bfloat16).at[send_index].set(child_slot.astype(jnp.bfloat16))
    )
    live_mask = jnp.arange(height_cap, dtype=jnp.int32)[None, :] < heights[0][:, None]
    own = jnp.where(live_mask[:, :, None], front_rows, jnp.zeros_like(front_rows))
    got_rows, got_front, got_slot = (
        lax.all_to_all(
            send_rows.reshape(peers, capacity, width),
            "rows",
            split_axis=0,
            concat_axis=0,
            tiled=True,
        ),
        lax.all_to_all(
            send_front.reshape(peers, capacity), "rows", split_axis=0, concat_axis=0, tiled=True
        ),
        lax.all_to_all(
            send_slot.reshape(peers, capacity), "rows", split_axis=0, concat_axis=0, tiled=True
        ),
    )
    got_rows = got_rows.reshape(slots, width)
    got_lead = got_rows[:, :NB]
    target = got_front.reshape(-1).astype(jnp.int32) * height_cap + got_slot.reshape(-1).astype(
        jnp.int32
    )
    placing = (jnp.arange(fronts * height_cap, dtype=jnp.int32)[:, None] == target[None, :]).astype(
        jnp.bfloat16
    )
    added = jnp.dot(placing, got_lead, preferred_element_type=jnp.float32)
    panel_local = (
        own[:, :, :NB].reshape(fronts * height_cap, NB).astype(jnp.float32) + added
    ).astype(jnp.bfloat16)
    panel = from_root(panel_local.reshape(fronts, height_cap, NB), "cols", 0)
    selected = jnp.dot(
        placing.T, panel.reshape(fronts * height_cap, NB), preferred_element_type=jnp.float32
    ).astype(jnp.bfloat16)
    which = (
        jnp.arange(fronts, dtype=jnp.int32)[:, None]
        == got_front.reshape(-1).astype(jnp.int32)[None, :]
    ).astype(jnp.bfloat16)
    picked = which[:, :, None] * selected[None, :, :]
    child_cross = jnp.einsum("fsk,sc->fkc", picked, got_rows, preferred_element_type=jnp.float32)
    gram = jnp.einsum("fhk,fhj->fkj", panel, panel, preferred_element_type=jnp.float32)
    share_width = width // peers
    cross = jnp.einsum("fhk,fhc->fkc", panel, own, preferred_element_type=jnp.float32) + child_cross
    cross_total, gram_total = lax.psum((cross, gram), "rows")
    start = lax.axis_index("rows") * share_width
    columns = lax.dynamic_slice_in_dim(cross_total, start, share_width, 2)
    lower = jnp.linalg.cholesky(gram_total)
    return jax.vmap(solve_block)(lower, columns)


def solution(mesh):
    placed = (
        P(None, "rows", "cols"),
        P("rows", None),
        P("rows", "cols"),
        P("rows", None),
        P("rows"),
        P("rows"),
    )
    return jax.shard_map(
        on_device,
        mesh=mesh,
        in_specs=placed,
        out_specs=P(None, None, ("cols", "rows")),
        check_vma=False,
    )
```

profile of v0, /device:TPU:8, one launch (start us, length us, event | category | flops | bytes accessed | tf_op | source)
XLA Modules:
  0.0 623.2 jit_solution(7834299393505477574)
XLA Ops:
  6.5 0.7 fusion.21
  7.2 18.0 %reduce-window.6 = s32[64,8,128]{2,1,0:T(8,128)S(1)} reduce-window(s32[64,8,128]{2,1,0:T(8,128)S(1)} %fusion.21, s32[]{:T(128)} %constant.64.clone.1), window={size=1x1x128 pad=0_0x0_0x127_0}, to_apply=%region_0.0 | reduce-window | flops 8323072 | bytes 524292 | tf_op jit(solution)/shard_map/reduce-window
  25.3 0.1 slice.29
  25.4 0.1 copy.37
  25.6 0.1 copy.38
  25.7 0.1 broadcast_add_fusion
  25.8 0.8 fusion.20
  26.6 0.7 compare_select_fusion
  27.3 0.7 broadcast_in_dim.25
  28.0 0.1 reshape.137
  28.1 4.3 scatter_custom_fusion
  32.4 0.7 all_to_all.20
  33.1 11.9 %all-to-all-start = ((bf16[64,1,32]{2,1,0:T(2,128)(2,1)}), bf16[64,1,32]{2,1,0:T(2,128)(2,1)S(1)}, u32[]{:S(2)}, u32[]{:S(2)}) async-start(bf16[64,1,32]{2,1,0:T(2,128)(2,1)} %all_to_all.20), calls=%async_computation | async-start | bytes 65536 | tf_op jit(solution)/shard_map/all_to_all | solution.py:47
  45.0 0.7 convert_element_type.64
  45.7 7.6 %scatter_custom_fusion.1 = bf16[2048]{0:T(1024)(128)(2,1)S(1)} fusion(s32[1024]{0:T(1024)S(1)} %bitcast.56, bf16[1024]{0:T(1024)(128)(2,1)S(1)} %convert_element_type.64, bf16[]{:T(256)} %constant.65.clone.1), kind=kCustom, calls=%fused_computation.48 | custom fusion | bytes 4098 | tf_op jit(solution)/shard_map/scatter | solution.py:35
  53.3 0.7 all_to_all.21
  54.0 0.6 all-to-all-done
  54.6 9.7 %all-to-all-start.1 = ((bf16[64,1,32]{2,1,0:T(2,128)(2,1)}), bf16[64,1,32]{2,1,0:T(2,128)(2,1)S(1)}, u32[]{:S(2)}, u32[]{:S(2)}) async-start(bf16[64,1,32]{2,1,0:T(2,128)(2,1)} %all_to_all.21), calls=%async_computation.1 | async-start | bytes 65536 | tf_op jit(solution)/shard_map/all_to_all | solution.py:50
  64.3 8.6 %scatter_custom_fusion.2 = bf16[2048,1024]{1,0:T(8,128)(2,1)} fusion(s32[1024]{0:T(1024)S(1)} %bitcast.57, bf16[1024,1024]{1,0:T(8,128)(2,1)} %param.8, bf16[]{:T(256)} %constant.65.clone.1), kind=kCustom, calls=%fused_computation.14 | custom fusion | bytes 4194816 | tf_op jit(solution)/shard_map/scatter | solution.py:31
  72.9 1.0 all-to-all-done.1
  73.9 0.0 copy-start.1
  73.9 9.7 %all-to-all-start.2 = ((bf16[64,32,1024]{2,1,0:T(8,128)(2,1)}), bf16[64,32,1024]{2,1,0:T(8,128)(2,1)}, u32[]{:S(2)}, u32[]{:S(2)}) async-start(bf16[64,32,1024]{2,1,0:T(8,128)(2,1)} %bitcast.46), calls=%async_computation.2 | async-start | bytes 8388608 | tf_op jit(solution)/shard_map/all_to_all | solution.py:40
  83.6 0.0 all-reduce.4.cloned.1.call-start
  83.7 0.0 copy-done.1
  83.7 0.1 iota_compare_fusion.16
  83.8 1.8 broadcast_select_fusion
  85.6 0.1 slice.28
  85.7 0.1 convert_reduce_fusion.1
  85.8 0.1 reshape.131
  85.9 0.1 convert_reduce_fusion
  86.0 0.1 reshape.132
  86.0 93.8 %all-to-all-done.2 = bf16[64,32,1024]{2,1,0:T(8,128)(2,1)} async-done(((bf16[64,32,1024]{2,1,0:T(8,128)(2,1)}), bf16[64,32,1024]{2,1,0:T(8,128)(2,1)}, u32[]{:S(2)}, u32[]{:S(2)}) %all-to-all-start.2) | async-done | bytes 4194336 | tf_op jit(solution)/shard_map/all_to_all | solution.py:40
  179.9 3.4 fusion.13
  183.3 0.0 all-reduce.4.cloned.1.call-update
  183.3 0.0 all-reduce.6.cloned.1.call-start
  183.4 42.1 %all-reduce.4.cloned.1.call-done = bf16[8,128,128]{2,1,0:T(8,128)(2,1)} async-done(((bf16[8,128,128]{2,1,0:T(8,128)(2,1)}), bf16[8,128,128]{2,1,0:T(8,128)(2,1)}) %all-reduce.4.cloned.1.call-update) | async-done | bytes 262160 | tf_op jit(solution)/shard_map/psum | solution.py:11
  225.5 3.3 fusion.6
  228.8 0.0 copy-start
  228.8 7.2 %fusion.2 = f32[8,128,1024]{1,2,0:T(8,128)S(1)} fusion(bf16[2048,1024,1]{1,0,2:T(8,128)(2,1)} %bitcast.15, bf16[2048,128]{1,0:T(8,128)(2,1)S(1)} %fusion.6, bf16[8,2048]{1,0:T(8,128)(2,1)S(1)} %fusion.23), kind=kOutput, calls=%fused_computation.6 | convolution fusion | flops 4297064448 | bytes 8945664 | tf_op jit(solution)/shard_map/fsk,sc->fkc/dot_general | solution.py:75
  236.0 0.0 copy-done
  236.1 1.1 fusion.29
  237.2 2.9 convolution_add_fusion
  240.1 0.0 all-reduce.6.cloned.1.call-update
  240.1 198.9 %all-reduce.6.cloned.1.call-done = (f32[8,128,128]{1,2,0:T(8,128)}, f32[8,128,1024]{1,2,0:T(8,128)}) async-done(((f32[8,128,128]{1,2,0:T(8,128)}, f32[8,128,1024]{1,2,0:T(8,128)}), (f32[8,128,128]{1,2,0:T(8,128)}, f32[8,128,1024]{1,2,0:T(8,128)})) %all-reduce.6.cloned.1.call-update) | async-done | bytes 4718608 | tf_op jit(solution)/shard_map/psum | solution.py:79
  439.1 1.2 copy.43
  440.3 1.1 fusion.17
  441.4 94.0 %custom-call.8 = f32[8,128,128]{2,1,0:T(8,128)S(1)} custom-call(f32[8,128,128]{2,1,0:T(8,128)S(1)} %fusion.17), custom_call_target="Cholesky" | custom-call | tf_op jit(solution)/shard_map/jit(cholesky)/cholesky | solution.py:82
  535.4 0.1 select_reduce_fusion
  535.5 0.1 compare_reduce_fusion
  535.6 0.1 select_bitcast_fusion
  535.7 78.6 %custom-call.9 = f32[8,1,128,128]{2,3,1,0:T(8,128)S(1)} custom-call(f32[8,1,128,128]{3,2,1,0:T(8,128)S(1)} %select_bitcast_fusion), custom_call_target="InvertDiagBlocksLowerTriangular" | custom-call | tf_op jit(solution)/shard_map/vmap(jit(_solve_triangular))/triangular_solve | solution.py:15
  614.3 2.0 fusion.15
  (7 shorter events, 0.1 us)
Async XLA Ops:
  33.1 21.6 %all-to-all-start = ((bf16[64,1,32]{2,1,0:T(2,128)(2,1)}), bf16[64,1,32]{2,1,0:T(2,128)(2,1)S(1)}, u32[]{:S(2)}, u32[]{:S(2)}) async-start(bf16[64,1,32]{2,1,0:T(2,128)(2,1)} %all_to_all.20), calls=%async_computation | async-start | bytes 65536 | tf_op jit(solution)/shard_map/all_to_all | solution.py:47
  54.6 19.2 %all-to-all-start.1 = ((bf16[64,1,32]{2,1,0:T(2,128)(2,1)}), bf16[64,1,32]{2,1,0:T(2,128)(2,1)S(1)}, u32[]{:S(2)}, u32[]{:S(2)}) async-start(bf16[64,1,32]{2,1,0:T(2,128)(2,1)} %all_to_all.21), calls=%async_computation.1 | async-start | bytes 65536 | tf_op jit(solution)/shard_map/all_to_all | solution.py:50
  73.9 9.8 %copy-start.1 = (s32[1,8]{1,0:T(1,128)S(1)}, s32[1,8]{1,0:T(1,128)}, u32[]{:S(2)}) copy-start(s32[1,8]{1,0:T(1,128)} %param.7) | copy-start | bytes 100
  73.9 106.0 %all-to-all-start.2 = ((bf16[64,32,1024]{2,1,0:T(8,128)(2,1)}), bf16[64,32,1024]{2,1,0:T(8,128)(2,1)}, u32[]{:S(2)}, u32[]{:S(2)}) async-start(bf16[64,32,1024]{2,1,0:T(8,128)(2,1)} %bitcast.46), calls=%async_computation.2 | async-start | bytes 8388608 | tf_op jit(solution)/shard_map/all_to_all | solution.py:40
  83.6 141.9 %all-reduce.4.cloned.1.call-start = ((), (), s32[]{:S(2)}) async-start(), calls=%async_computation.3 | async-start | bytes 524288 | tf_op jit(solution)/shard_map/psum | solution.py:11
  183.3 255.8 %all-reduce.6.cloned.1.call-start = ((), (), s32[]{:S(2)}) async-start(), calls=%async_computation.4 | async-start | bytes 9437184 | tf_op jit(solution)/shard_map/psum | solution.py:79
  228.8 7.3 %copy-start = (bf16[8,128,128]{2,1,0:T(8,128)(2,1)S(1)}, bf16[8,128,128]{2,1,0:T(8,128)(2,1)}, u32[]{:S(2)}) copy-start(bf16[8,128,128]{2,1,0:T(8,128)(2,1)} %all-reduce.4.cloned.1.call-done) | copy-start | bytes 786436
Sparse Core Ops, SparseCore 0:
  183.4 42.0 all-reduce.3
  240.2 198.7 all-reduce.5
where the time goes:
time: 624 us; the launch traced here: 623 us
  waiting for transfers between devices  336 us (54%)
  other arithmetic  197 us (32%)
  starting transfers between devices  31.4 us (5%)
  local copies, waits for them, and re-layouts  24.5 us (4%)
  matrix products  20 us (3%)
  between operations  13.6 us (2%)
    psum x1, waiting for transfers between devices, on_device(): cross_total, gram_total = lax.psum((cross, gram), 'rows')  199 us
    another operation x4, other arithmetic, on_device(): lower = jnp.linalg.cholesky(gram_total)  94.2 us
    all_to_all x1, waiting for transfers between devices, on_device(): lax.all_to_all(send_rows.reshape(peers, capacity, width), 'rows', split_a...  93.8 us
    another operation x3, other arithmetic, solve_block(): return jax.scipy.linalg.solve_triangular(lower, columns, lower=True)  78.7 us
    psum x1, waiting for transfers between devices, from_root(): return lax.psum(block, axis)  42.1 us
    another operation x3, other arithmetic  18.2 us
  transfers between devices with their start and end apart: 5, of which 5 were waited for; matrix products, arithmetic and copies ran while one was open for 3% of the time, Pallas kernels for 0%

commit v1 on v0

v1 whole, which is shorter than its diff:
```python
import jax
import jax.numpy as jnp
from jax import lax
from jax.experimental import pallas as pl
from jax.experimental.pallas import tpu as pltpu
from jax.sharding import PartitionSpec as P

NB = 128
CORES = 2
X = 4
BF = jnp.bfloat16
F32 = jnp.float32
I32 = jnp.int32


def dot(a, b, ca, cb, precision=None):
    return lax.dot_general(
        a, b, (((ca,), (cb,)), ((), ())), precision=precision, preferred_element_type=F32
    )


def iota(shape, axis):
    return lax.broadcasted_iota(I32, shape, axis)


def onehot(mask):
    return jnp.where(mask, 1.0, 0.0).astype(BF)


def vmem(n):
    return [pl.BlockSpec(memory_space=pltpu.VMEM)] * n


def call(kernel, outs, in_specs, scratch=(), flops=1 << 20, name=None):
    return pl.pallas_call(
        kernel,
        out_shape=outs,
        in_specs=in_specs,
        out_specs=jax.tree.map(lambda _: pl.BlockSpec(memory_space=pltpu.VMEM), outs),
        scratch_shapes=scratch,
        cost_estimate=pl.CostEstimate(flops=flops, bytes_accessed=1 << 20, transcendentals=0),
        name=name,
    )


SMEM = pl.BlockSpec(memory_space=pltpu.SMEM)


def lead_kernel(child_ref, front_ref, heights_ref, out_ref):
    eye = onehot(iota((NB, NB), 0) == iota((NB, NB), 1))
    quarter = out_ref.shape[1] // 2
    child = dot(eye, child_ref[...], 1, 1).astype(BF)
    for c in range(out_ref.shape[0]):
        out_ref[c, :quarter] = child[c * quarter : (c + 1) * quarter]
    for f in range(front_ref.shape[0]):
        own = dot(eye, front_ref[f], 1, 1)
        own = jnp.where(iota(own.shape, 1) < heights_ref[0, f], own, 0.0).astype(BF)
        for c in range(out_ref.shape[0]):
            out_ref[c, quarter:, f * NB : (f + 1) * NB] = own[c * quarter : (c + 1) * quarter]


def index_kernel(peers, capacity, groups, dest_ref, key_ref):
    count = dest_ref.shape[1]
    dest = dest_ref[...]
    hits = onehot(iota((peers, count), 0) == dest)
    upper = onehot(iota((NB, NB), 0) < iota((NB, NB), 1))
    offset = jnp.zeros((peers, 1), F32)
    per = capacity // groups
    for b in range(count // NB):
        block = hits[:, b * NB : (b + 1) * NB]
        before = dot(block, upper, 1, 0) + offset
        block = block.astype(F32)
        position = jnp.sum(before * block, axis=0, keepdims=True).astype(I32)
        offset = offset + jnp.sum(block, axis=1, keepdims=True)
        where_to = dest[:, b * NB : (b + 1) * NB]
        key_ref[:, b * NB : (b + 1) * NB] = (
            (position // per) * (peers * per) + where_to * per + position % per
        )


def quarter_of(col, parts, low, high):
    base = parts[0][0, low:high].astype(F32)
    total = jnp.where(col == 0, base, jnp.zeros_like(base))
    for part in parts[1:]:
        total = total + part[low:high].astype(F32)
    return total


def placed(block, q, groups):
    rows = block.shape[0]
    pieces = []
    if q:
        pieces.append(jnp.zeros((q * rows, block.shape[1]), block.dtype))
    pieces.append(block)
    if q < groups - 1:
        pieces.append(jnp.zeros(((groups - 1 - q) * rows, block.shape[1]), block.dtype))
    return jnp.concatenate(pieces, axis=0)


def pack_kernel(col_ref, parent_ref, key_ref, slot_ref, p0, p1, p2, p3, out_ref):
    groups = 4
    quarter = NB // groups
    count = key_ref.shape[1]
    peers = out_ref.shape[0]
    per = out_ref.shape[1] // 2
    lead = quarter_of(col_ref[0], (p0, p1, p2, p3), 0, quarter).astype(BF)
    lane = iota((1, count), 1)
    kb = count // parent_ref.shape[0]
    front = jnp.zeros((1, count), I32)
    for b in range(parent_ref.shape[0]):
        front = jnp.where(lane // kb == b, parent_ref[b], front)
    slot = slot_ref[...].astype(F32)
    front = front.astype(F32)
    key = key_ref[...]
    total = jnp.zeros((peers * per, 2 * NB), F32)
    rows = iota((NB, count), 0)
    for q in range(groups):
        meta = jnp.where(rows == q, slot, jnp.where(rows == groups + q, front, 0.0)).astype(BF)
        source = jnp.concatenate([placed(lead, q, groups), meta], axis=0)
        hit = onehot(iota((peers * per, count), 0) + q * peers * per == key)
        total = total + dot(hit, source, 1, 1)
    data = total[:, :NB].reshape(peers, per, NB)
    meta = total[:, NB:].reshape(peers, per, NB)
    out_ref[...] = jnp.concatenate([data, meta], axis=1).astype(BF)


def panel_kernel(col_ref, got_ref, p0, p1, p2, p3, panel_ref, back_ref, hit_ref):
    groups = 4
    quarter = NB // groups
    peers, twice, _ = got_ref.shape
    per = twice // 2
    targets = panel_ref.shape[1]
    got = got_ref[...].astype(F32)
    data = got[:, :per].reshape(peers * per, NB)
    meta = got[:, per:].reshape(peers * per, NB)
    target = (meta + NB * pltpu.roll(meta, NB - groups, 1)).astype(I32)
    turned = data.T.astype(BF)
    total = quarter_of(col_ref[0], (p0, p1, p2, p3), quarter, 2 * quarter)
    for q in range(groups):
        hit_ref[q] = onehot(iota((peers * per, targets), 1) == target[:, q : q + 1])
        total = total + dot(turned[q * quarter : (q + 1) * quarter], hit_ref[q], 1, 0)
    panel = total.astype(BF)
    panel_ref[...] = panel
    back = jnp.zeros((peers * per, NB), F32)
    for q in range(groups):
        back = back + dot(hit_ref[q], placed(panel, q, groups), 1, 1)
    back_ref[...] = back.reshape(peers, per, NB).astype(BF)


def pick_kernel(key_ref, got_ref, out_ref):
    groups = 4
    quarter = NB // groups
    peers, per, _ = got_ref.shape
    count = key_ref.shape[1]
    turned = got_ref[...].astype(F32).reshape(peers * per, NB).T.astype(BF)
    key = key_ref[...]
    total = jnp.zeros((quarter, count), F32)
    for q in range(groups):
        hit = onehot(iota((peers * per, count), 0) + q * peers * per == key)
        total = total + dot(turned[q * quarter : (q + 1) * quarter], hit, 1, 0)
    out_ref[...] = total.astype(BF)


def turn_kernel(core_ref, child_ref, front_ref, out_ref):
    halves, xs, zs, run, _ = out_ref.shape
    row, column = iota((NB, NB), 0), iota((NB, NB), 1)
    half = row // (xs * run)
    core = jnp.where(half == 0, 1 - core_ref[0], core_ref[0])
    pick = onehot(column == ((row // run) % xs) * (CORES * run) + core * run + row % run)
    count = child_ref.shape[0]
    for z in range(zs):
        turned = dot(pick, child_ref[:, z * NB : (z + 1) * NB], 1, 1).astype(BF)
        own = [
            dot(pick, front_ref[f, :, z * NB : (z + 1) * NB], 1, 1).astype(BF)
            for f in range(front_ref.shape[0])
        ]
        turned = jnp.concatenate(own + [turned], axis=1)
        for h in range(halves):
            for x in range(xs):
                low = (h * xs + x) * run
                out_ref[h, x, z] = turned[low : low + run]


def ring_into(col, parts, whole):
    n = len(parts)
    for d in range(n):
        whole[lax.rem(col - d + n, n)] = parts[d][...]


def cross_kernel(
    half, col_ref, parent_ref, heights_ref, rows_ref,
    a0, a1, a2, a3, b0, b1, b2, b3, out_ref, panel_ref, picked_ref
):
    fronts = heights_ref.shape[1]
    col = col_ref[0]
    ring_into(col, (a0, a1, a2, a3), panel_ref)
    ring_into(col, (b0, b1, b2, b3), picked_ref)
    count = picked_ref.shape[2]
    own = fronts * NB
    panel = panel_ref[...].reshape(NB, own)
    picked = picked_ref[...].reshape(NB, count)
    kb = count // parent_ref.shape[0]
    lane = iota((1, count), 1) // kb
    front = jnp.zeros((1, count), I32)
    for b in range(parent_ref.shape[0]):
        front = jnp.where(lane == b, parent_ref[b], front)
    height = iota((NB, NB), 1)
    rows = rows_ref[...].reshape(-1, own + count)
    zero = jnp.zeros((NB, NB), BF)
    for f in range(0, fronts, 2):
        owns, kids = [], []
        for g in (f, f + 1):
            block = panel[:, g * NB : (g + 1) * NB]
            block = jnp.where(height < heights_ref[0, g], block, zero)
            owns.append(jnp.concatenate([block, zero] if g == f else [zero, block], axis=1))
            kids.append(jnp.where(front == g, picked, jnp.zeros_like(picked)))
        weights = jnp.concatenate(
            [jnp.concatenate(owns, axis=0), jnp.concatenate(kids, axis=0)], axis=1
        )
        left = jnp.concatenate([rows[:, f * NB : (f + 2) * NB], rows[:, own:]], axis=1)
        out_ref[:, f * NB : (f + 2) * NB] = dot(left, weights, 1, 1)


def gram_kernel(col_ref, a0, a1, a2, a3, out_ref, panel_ref):
    ring_into(col_ref[0], (a0, a1, a2, a3), panel_ref)
    panel = panel_ref[...].reshape(NB, panel_ref.shape[2])
    for f in range(out_ref.shape[0] // NB):
        block = panel[:, f * NB : (f + 1) * NB]
        out_ref[f * NB : (f + 1) * NB] = dot(block, block, 1, 1)


def factor_kernel(gram_ref, out_ref, a_ref):
    n = gram_ref.shape[0]
    row, column = iota((NB, NB), 0), iota((NB, NB), 1)
    for f in range(n):
        a_ref[f] = gram_ref[f]
        out_ref[f] = jnp.where(row == column, 1.0, 0.0)

    def block(t, carry):
        for j in range(8):
            for f in range(n):
                a = a_ref[f]
                pivot_rows = a_ref[f, pl.ds(t * 8, 8), :]
                pivot_row = pivot_rows[j : j + 1]
                inverse_rows = out_ref[f, pl.ds(t * 8, 8), :]
                inverse_row = inverse_rows[j : j + 1]
                factor = a[:, j : j + 1] * (1.0 / pivot_row[:, j : j + 1])
                factor = jnp.where(row[:, :1] > t * 8 + j, factor, 0.0)
                a_ref[f] = a - factor * pivot_row
                out_ref[f] = out_ref[f] - factor * inverse_row
        for f in range(n):
            rows = a_ref[f, pl.ds(t * 8, 8), :]
            eye = iota((8, NB), 0) == iota((8, NB), 1)
            d = jnp.sum(jnp.where(eye, rows, 0.0), axis=1, keepdims=True)
            out_ref[f, pl.ds(t * 8, 8), :] = out_ref[f, pl.ds(t * 8, 8), :] * lax.rsqrt(d)
            a_ref[f] = pltpu.roll(a_ref[f], NB - 8, 1)
        return carry

    lax.fori_loop(0, NB // 8, block, 0)


def solve_kernel(col_ref, cross_ref, i0, i1, i2, i3, out_ref, inverse_ref):
    ring_into(col_ref[0], (i0, i1, i2, i3), inverse_ref)
    total = jnp.sum(cross_ref[...], axis=0)
    n = inverse_ref.shape[1]
    for f in range(out_ref.shape[0]):
        out_ref[f] = dot(
            total[:, f * NB : (f + 1) * NB], inverse_ref[f // n, f % n], 1, 1,
            precision=lax.Precision.HIGHEST,
        )


def on_device(front_rows, heights, child_rows, child_dest, child_slot, parent_ids):
    fronts, height_cap, width = front_rows.shape
    peers = lax.axis_size("rows")
    cols = lax.axis_size("cols")
    count = child_rows.shape[0]
    zs = peers // (X * CORES)
    capacity = max(2, 2 * count // peers)
    quarter = NB // cols
    per = capacity * quarter // NB
    run = width // peers
    targets = fronts * height_cap
    sds = jax.ShapeDtypeStruct

    col = lax.axis_index("cols")[None]
    core = (lax.axis_index("rows") % CORES)[None]

    def spread(value, shifts=range(1, 4)):
        return [value] + [
            lax.ppermute(value, "cols", [(i, (i + d) % cols) for i in range(cols)])
            for d in shifts
        ]

    dest = child_dest.reshape(1, count)
    slot = child_slot.reshape(1, count)

    lead = pl.pallas_call(
        lead_kernel,
        grid=(1,),
        out_shape=sds((cols, 2 * quarter, count), BF),
        in_specs=[
            pl.BlockSpec((count, NB), lambda i: (0, 0)),
            pl.BlockSpec((fronts, height_cap, NB), lambda i: (0, 0, 0)),
            SMEM,
        ],
        out_specs=pl.BlockSpec((cols, 2 * quarter, count), lambda i: (0, 0, 0)),
        name="lead",
    )(child_rows, front_rows, heights)
    parts = [lead] + [lax.ppermute(lead[d], "cols", [(0, d)]) for d in range(1, cols)]

    key = call(
        lambda *r: index_kernel(peers, capacity, cols, *r), sds((1, count), I32), vmem(1),
        name="index",
    )(dest)
    send = call(
        pack_kernel, sds((peers, 2 * per, NB), BF), [SMEM, SMEM] + vmem(6), name="pack"
    )(col, parent_ids, key, slot, *parts)
    got = lax.all_to_all(send, "rows", 0, 0, tiled=True)

    rows = call(
        turn_kernel, sds((CORES, X, zs, run, targets + count), BF), [SMEM] + vmem(2),
        flops=1 << 29, name="turn",
    )(core, child_rows, front_rows)

    panel, back = call(
        panel_kernel,
        (sds((quarter, targets), BF), sds((peers, per, NB), BF)),
        [SMEM] + vmem(5),
        [pltpu.VMEM((cols, peers * per, targets), BF)],
        name="panel",
    )(col, got, *parts)
    returned = lax.all_to_all(back, "rows", 0, 0, tiled=True)
    panels = spread(panel)

    whole = [pltpu.VMEM((cols, quarter, targets), BF)]
    gram = call(gram_kernel, sds((fronts * NB, NB), F32), [SMEM] + vmem(4), whole, name="gram")(
        col, *panels
    )
    share = fronts // cols * NB
    mine = lax.dynamic_slice_in_dim(gram, col[0] * share, share, 0)
    sums = lax.all_to_all(mine.reshape(peers, share // peers, NB), "rows", 0, 0, tiled=True)
    sums = jnp.sum(sums, axis=0)
    sums = lax.all_to_all(
        jnp.broadcast_to(sums[None], (peers, share // peers, NB)), "rows", 0, 0, tiled=True
    )
    inverse = call(
        factor_kernel, sds((fronts // cols, NB, NB), F32), vmem(1),
        [pltpu.VMEM((fronts // cols, NB, NB), F32)], flops=1 << 28, name="factor",
    )(sums.reshape(fronts // cols, NB, NB))
    inverses = spread(inverse)

    picked = call(pick_kernel, sds((quarter, count), BF), vmem(2), name="pick")(key, returned)
    pickeds = spread(picked)

    halves = []
    for h in range(CORES):
        halves.append(
            call(
                lambda *r, h=h: cross_kernel(h, *r),
                sds((X * zs * run, targets), F32),
                [SMEM, SMEM, SMEM] + vmem(9),
                [
                    pltpu.VMEM((cols, quarter, targets), BF),
                    pltpu.VMEM((cols, quarter, count), BF),
                ],
                flops=1 << 31,
                name="cross%d" % h,
            )(col, parent_ids, heights, rows[h], *panels, *pickeds)
        )
    other = lax.ppermute(halves[0], "rows", [(i, i ^ 1) for i in range(peers)])
    chip = (halves[1] + other).reshape(X, zs * run, targets)

    def at(z, x, c):
        return (z * X + x) * CORES + c

    over_x = [[at(z, x, c) for x in range(X)] for z in range(zs) for c in range(CORES)]
    over_z = [[at(z, x, c) for z in range(zs)] for x in range(X) for c in range(CORES)]
    chip = lax.all_to_all(chip, "rows", 0, 0, axis_index_groups=over_x, tiled=True)
    chip = jnp.sum(chip, axis=0).reshape(zs, run, targets)
    chip = lax.all_to_all(chip, "rows", 0, 0, axis_index_groups=over_z, tiled=True)

    out = call(
        solve_kernel, sds((fronts, run, NB), F32), [SMEM] + vmem(5),
        [pltpu.VMEM((cols, fronts // cols, NB, NB), F32)], name="solve",
    )(col, chip, *inverses)
    return jnp.transpose(out, (0, 2, 1))


def solution(mesh):
    placed_as = (
        P(None, "rows", "cols"),
        P("rows", None),
        P("rows", "cols"),
        P("rows", None),
        P("rows"),
        P("rows"),
    )
    return jax.shard_map(
        on_device,
        mesh=mesh,
        in_specs=placed_as,
        out_specs=P(None, None, ("cols", "rows")),
        check_vma=False,
    )
```

time: 624 us -> 201 us (0.32)
  waiting for transfers between devices: 336 us -> 50.3 us
  other arithmetic: 197 us -> 4.37 us
  Pallas kernels: 0 us -> 62.5 us
  blocking collectives: 0 us -> 24.9 us
  matrix products: 20 us -> 0 us
  starting transfers between devices: 31.4 us -> 46.3 us
  between operations: 13.6 us -> 0.2 us
  local copies, waits for them, and re-layouts: 24.5 us -> 11.6 us
    psum x2 -> x0, waiting for transfers between devices: 241 us -> none  [the longest x1 199 us: on_device(): cross_total, gram_total = lax.psum((cross, gram), 'rows')]
    another operation x10 -> x0, other arithmetic: 191 us -> none  [the longest x4 94.2 us: on_device(): lower = jnp.linalg.cholesky(gram_total)]
    pallas_call x0 -> x11, Pallas kernels: none -> 62.5 us  [the longest x1 27.8 us: on_device(): call(factor_kernel, sds((fronts // cols, NB, NB), F32), vmem(1), [pltpu.V...]
    all_to_all x3 -> x5, waiting for transfers between devices: 95.4 us -> 39.9 us  [the longest x1 26.8 us: on_device(): lax.all_to_all(chip, 'rows', 0, 0, axis_index_groups=over_x, tiled=True)]
    all_to_all x0 -> x1, blocking collectives: none -> 24.9 us  [on_device(): got = lax.all_to_all(send, 'rows', 0, 0, tiled=True)]
    scatter x3 -> x0, local copies, waits for them, and re-layouts: 20.5 us -> none  [the longest x1 8.6 us: on_device(): jnp.zeros((slots, width), jnp.bfloat16).at[send_index].set(child_rows)]
    ppermute x0 -> x13, starting transfers between devices: none -> 19.6 us  [the longest x9 17 us: spread(): lax.ppermute(value, 'cols', [(i, (i + d) % cols) for i in range(cols)])]
    dot_general x5 -> x0, matrix products: 18 us -> none  [the longest x1 7.24 us: on_device(): jnp.einsum('fsk,sc->fkc', picked, got_rows, preferred_element_type=jnp.fl...]
  transfers between devices with their start and end apart: 5 -> 18, of which waited for: 5 -> 7; matrix products, arithmetic and copies ran while one was open for 3% -> 5% of each run, Pallas kernels for 0% -> 23%
where the time goes in v1:
time: 201 us; the launch traced here: 200 us
  Pallas kernels  62.5 us (31%)
  waiting for transfers between devices  50.3 us (25%)
  starting transfers between devices  46.3 us (23%)
  blocking collectives  24.9 us (12%)
  local copies, waits for them, and re-layouts  11.6 us (6%)
  other arithmetic  4.37 us (2%)
    pallas_call x1, Pallas kernels, on_device(): call(factor_kernel, sds((fronts // cols, NB, NB), F32), vmem(1), [pltpu.V...  27.8 us
    all_to_all x1, waiting for transfers between devices, on_device(): lax.all_to_all(chip, 'rows', 0, 0, axis_index_groups=over_x, tiled=True)  26.8 us
    all_to_all x1, blocking collectives, on_device(): got = lax.all_to_all(send, 'rows', 0, 0, tiled=True)  24.9 us
    ppermute x9, starting transfers between devices, spread(): lax.ppermute(value, 'cols', [(i, (i + d) % cols) for i in range(cols)])  17 us
    all_to_all x1, waiting for transfers between devices, on_device(): lax.all_to_all(jnp.broadcast_to(sums[None], (peers, share // peers, NB)),...  10.1 us
    pallas_call x2, Pallas kernels, on_device(): call(lambda *r, h=h: cross_kernel(h, *r), sds((X * zs * run, targets), F3...  9.36 us
    all_to_all x1, starting transfers between devices, on_device(): lax.all_to_all(mine.reshape(peers, share // peers, NB), 'rows', 0, 0, til...  8.81 us
    ppermute x9, waiting for transfers between devices, spread(): lax.ppermute(value, 'cols', [(i, (i + d) % cols) for i in range(cols)])  6.98 us
  transfers between devices with their start and end apart: 18, of which 7 were waited for; matrix products, arithmetic and copies ran while one was open for 5% of the time, Pallas kernels for 23%

profile of v1, /device:TPU:8, one launch (start us, length us, event | category | flops | bytes accessed | tf_op | source)
XLA Modules:
  0.0 200.2 jit_solution(17862451088687540918)
XLA Ops:
  0.0 2.2 %lead.1.p0 = bf16[4,64,1024]{2,1,0:T(8,128)(2,1)} custom-call(bf16[1024,1024]{1,0:T(8,128)(2,1)} %child_ref.3, bf16[8,128,1024]{2,1,0:T(8,128)(2,1)} %front_ref.3, s32[1,8]{1,0:T(1,128)} %r_2_.3), custom_call_target="tpu_custom_call" | custom-call | tf_op jit(solution)/shard_map/lead/pallas_call | solution.py:298
  2.2 1.1 slice_bitcast_fusion.2
  3.3 1.3 collective-permute-start
  4.6 0.7 collective-permute-start.1
  5.3 0.7 collective-permute-start.2
  5.9 1.5 index.1.key_ref
  7.4 3.5 %collective-permute-done.p1 = bf16[64,1024]{1,0:T(8,128)(2,1)S(1)} collective-permute-done((bf16[64,1024]{1,0:T(8,128)(2,1)S(1)}, bf16[64,1024]{1,0:T(8,128)(2,1)S(1)}, u32[]{:S(2)}, u32[]{:S(2)}) %collective-permute-start) | collective-permute-done | bytes 131104 | tf_op jit(solution)/shard_map/ppermute | solution.py:310
  10.9 0.0 collective-permute-done.1.p2
  10.9 0.6 copy-done.2
  11.6 0.1 copy-done.3
  11.6 0.0 copy-done.4
  11.7 3.2 %pack.1 = bf16[64,16,128]{2,1,0:T(8,128)(2,1)} custom-call(s32[1]{0:T(128)} %bitcast.col_ref.r_0_, s32[16]{0:T(128)} %r_1_.3, s32[1,1024]{1,0:T(1,128)} %index.1.key_ref, s32[1,1024]{1,0:T(1,128)} %bitcast.20, bf16[4,64,1024]{2,1,0:T(8,128)(2,1)} %lead.1.p0, bf16[64,1024]{1,0:T(8,128)(2,1)} %copy-done.2, bf16[64,1024]{1,0:T(8,128)(2,1)} %copy-done.3, ...), custom_call_target="tpu_custom_call" | custom-call | flops 1048576 | bytes 1048576 | tf_op jit(solution)/shard_map/pack/pallas_call | solution.py:316
  14.8 24.9 %all_to_all.30.got_ref = bf16[64,16,128]{2,1,0:T(8,128)(2,1)} all-to-all(bf16[64,16,128]{2,1,0:T(8,128)(2,1)} %pack.1), channel_id=1, replica_groups=mesh['rows'=64,'cols'=4] {'rows'}, dimensions={0} | all-to-all | bytes 524288 | tf_op jit(solution)/shard_map/all_to_all | solution.py:319
  39.8 4.5 %panel.1 = (bf16[32,1024]{1,0:T(8,128)(2,1)}, bf16[64,8,128]{2,1,0:T(8,128)(2,1)}) custom-call(s32[1]{0:T(128)} %bitcast.col_ref.r_0_, bf16[64,16,128]{2,1,0:T(8,128)(2,1)} %all_to_all.30.got_ref, bf16[4,64,1024]{2,1,0:T(8,128)(2,1)} %lead.1.p0, bf16[64,1024]{1,0:T(8,128)(2,1)} %copy-done.2, bf16[64,1024]{1,0:T(8,128)(2,1)} %copy-done.3, ...), custom_call_target="tpu_custom_call" | custom-call | flops 1048576 | bytes 1048576 | tf_op jit(solution)/shard_map/panel/pallas_call | solution.py:326
  44.3 5.0 %all-to-all-start.1 = ((bf16[64,8,128]{2,1,0:T(8,128)(2,1)}), bf16[64,8,128]{2,1,0:T(8,128)(2,1)S(1)}, u32[]{:S(2)}, u32[]{:S(2)}) async-start(bf16[64,8,128]{2,1,0:T(8,128)(2,1)} %get-tuple-element.8), calls=%async_computation.1 | async-start | bytes 262144 | tf_op jit(solution)/shard_map/all_to_all | solution.py:333
  49.3 3.8 %collective-permute-start.3 = (bf16[32,1024]{1,0:T(8,128)(2,1)}, bf16[32,1024]{1,0:T(8,128)(2,1)S(1)}, u32[]{:S(2)}, u32[]{:S(2)}) collective-permute-start(bf16[32,1024]{1,0:T(8,128)(2,1)} %get-tuple-element.7.r_4_.a0), channel_id=1, source_target_pairs={{0,1},{1,2},{2,3},{3,0},{4,5},{5,6},{6,7},{7,4},{8,9},{9,10},{10,1... | collective-permute-start | bytes 196616 | tf_op jit(solution)/shard_map/ppermute | solution.py:291
  53.1 6.5 %turn.1 = bf16[2,4,8,16,2048]{4,3,2,1,0:T(8,128)(2,1)} custom-call(s32[1]{0:T(128)} %bitcast.1.core_ref, bf16[1024,1024]{1,0:T(8,128)(2,1)} %child_ref.3, bf16[8,128,1024]{2,1,0:T(8,128)(2,1)} %front_ref.3), custom_call_target="tpu_custom_call" | custom-call | flops 536870912 | bytes 1048576 | tf_op jit(solution)/shard_map/turn/pallas_call | solution.py:321
  59.6 1.4 collective-permute-start.4
  61.0 2.6 %collective-permute-start.5 = (bf16[32,1024]{1,0:T(8,128)(2,1)S(1)}, bf16[32,1024]{1,0:T(8,128)(2,1)S(1)}, u32[]{:S(2)}, u32[]{:S(2)}) collective-permute-start(bf16[32,1024]{1,0:T(8,128)(2,1)S(1)} %copy-done.9), channel_id=1, source_target_pairs={{0,3},{1,0},{2,1},{3,2},{4,7},{5,4},{6,5},{7,6},{8,11},{9,8},{10,9... | collective-permute-start | bytes 196616 | tf_op jit(solution)/shard_map/ppermute | solution.py:291
  63.6 0.0 all-to-all-done.1.got_ref
  63.6 0.6 copy-done.1
  64.3 2.4 %pick.1.r_8_ = bf16[32,1024]{1,0:T(8,128)(2,1)} custom-call(s32[1,1024]{1,0:T(1,128)} %index.1.key_ref, bf16[64,8,128]{2,1,0:T(8,128)(2,1)} %copy-done.1), custom_call_target="tpu_custom_call" | custom-call | flops 1048576 | bytes 1048576 | tf_op jit(solution)/shard_map/pick/pallas_call | solution.py:353
  66.7 0.4 collective-permute-start.6
  67.1 2.4 %collective-permute-start.7 = (bf16[32,1024]{1,0:T(8,128)(2,1)}, bf16[32,1024]{1,0:T(8,128)(2,1)S(1)}, u32[]{:S(2)}, u32[]{:S(2)}) collective-permute-start(bf16[32,1024]{1,0:T(8,128)(2,1)} %pick.1.r_8_), channel_id=1, source_target_pairs={{0,2},{1,3},{2,0},{3,1},{4,6},{5,7},{6,4},{7,5},{8,10},{9,11},{10,... | collective-permute-start | bytes 196616 | tf_op jit(solution)/shard_map/ppermute | solution.py:291
  69.4 0.0 collective-permute-done.3.r_5_.a1
  69.4 1.6 collective-permute-start.8
  71.1 4.8 %slice_bitcast_fusion = (bf16[4,8,16,2048]{3,2,1,0:T(8,128)(2,1)}, bf16[4,8,16,2048]{3,2,1,0:T(8,128)(2,1)}) fusion(bf16[2,4,8,16,2048]{4,3,2,1,0:T(8,128)(2,1)} %turn.1), kind=kLoop, calls=%fused_computation | loop fusion | bytes 8388608 | tf_op jit(solution)/shard_map/squeeze | solution.py:369
  75.9 0.0 collective-permute-done.4.r_6_.a2
  75.9 0.0 collective-permute-done.5.r_7_.a3
  75.9 0.0 collective-permute-done.6.r_9_
  76.0 0.0 collective-permute-done.8.r_11_
  76.0 0.5 copy-done.11
  76.5 0.0 copy-done.12
  76.6 0.0 copy-done.13
  76.6 0.0 copy-done.14
  76.6 0.0 copy-done.15
  76.6 4.7 %cross0.1 = f32[512,1024]{1,0:T(8,128)} custom-call(s32[1]{0:T(128)} %bitcast.col_ref.r_0_, s32[16]{0:T(128)} %r_1_.3, s32[1,8]{1,0:T(1,128)} %r_2_.3, bf16[4,8,16,2048]{3,2,1,0:T(8,128)(2,1)} %get-tuple-element.9.r_3_, bf16[32,1024]{1,0:T(8,128)(2,1)} %get-tuple-element.7.r_4_.a0, bf16[32,1024]{1,0:T(8,128)(2,1)} %copy-done.10, ...), custom_call_target="tpu_custom_call" | custom-call | flops 2147483648 | bytes 1048576 | tf_op jit(solution)/shard_map/cross0/pallas_call | solution.py:359
  81.3 0.0 collective-permute-start.9
  81.3 2.1 %gram.1 = f32[1024,128]{1,0:T(8,128)} custom-call(s32[1]{0:T(128)} %bitcast.col_ref.r_0_, bf16[32,1024]{1,0:T(8,128)(2,1)} %get-tuple-element.7.r_4_.a0, bf16[32,1024]{1,0:T(8,128)(2,1)} %copy-done.10, bf16[32,1024]{1,0:T(8,128)(2,1)} %copy-done.11, bf16[32,1024]{1,0:T(8,128)(2,1)} %copy-done.12), custom_call_target="tpu_custom_call" | custom-call | flops 1048576 | bytes 1048576 | tf_op jit(solution)/shard_map/gram/pallas_call | solution.py:337
  83.4 1.6 constant_dynamic-slice_fusion
  85.0 8.8 %all-to-all-start.4 = ((f32[64,4,128]{2,1,0:T(4,128)}), f32[64,4,128]{2,1,0:T(4,128)S(1)}, u32[]{:S(2)}, u32[]{:S(2)}) async-start(f32[64,4,128]{2,1,0:T(4,128)} %bitcast.11), calls=%async_computation.4 | async-start | bytes 262144 | tf_op jit(solution)/shard_map/all_to_all | solution.py:342
  93.8 4.7 %cross1.1 = f32[512,1024]{1,0:T(8,128)} custom-call(s32[1]{0:T(128)} %bitcast.col_ref.r_0_, s32[16]{0:T(128)} %r_1_.3, s32[1,8]{1,0:T(1,128)} %r_2_.3, bf16[4,8,16,2048]{3,2,1,0:T(8,128)(2,1)} %get-tuple-element.10.r_3_, bf16[32,1024]{1,0:T(8,128)(2,1)} %get-tuple-element.7.r_4_.a0, bf16[32,1024]{1,0:T(8,128)(2,1)} %copy-done.10, ...), custom_call_target="tpu_custom_call" | custom-call | flops 2147483648 | bytes 1048576 | tf_op jit(solution)/shard_map/cross1/pallas_call | solution.py:359
  98.5 0.0 collective-permute-done.9
  98.5 3.3 %add.11 = f32[512,1024]{1,0:T(8,128)} add(f32[512,1024]{1,0:T(8,128)} %cross1.1, f32[512,1024]{1,0:T(8,128)S(1)} %collective-permute-done.9) | non-fusion elementwise | flops 524288 | bytes 6291456 | tf_op jit(solution)/shard_map/add | solution.py:372
  101.8 3.0 %all-to-all-done.4 = f32[64,4,128]{2,1,0:T(4,128)S(1)} async-done(((f32[64,4,128]{2,1,0:T(4,128)}), f32[64,4,128]{2,1,0:T(4,128)S(1)}, u32[]{:S(2)}, u32[]{:S(2)}) %all-to-all-start.4) | async-done | bytes 131104 | tf_op jit(solution)/shard_map/all_to_all | solution.py:342
  104.8 3.6 %all-to-all-start.2 = ((f32[4,128,1024]{2,1,0:T(8,128)}), f32[4,128,1024]{2,1,0:T(8,128)S(1)}, u32[]{:S(2)}, u32[]{:S(2)}) async-start(f32[4,128,1024]{2,1,0:T(8,128)} %bitcast.9), calls=%async_computation.2 | async-start | bytes 4194304 | tf_op jit(solution)/shard_map/all_to_all | solution.py:379
  108.5 0.1 reduce_sum.19
  108.5 26.8 %all-to-all-done.2 = f32[4,128,1024]{2,1,0:T(8,128)S(1)} async-done(((f32[4,128,1024]{2,1,0:T(8,128)}), f32[4,128,1024]{2,1,0:T(8,128)S(1)}, u32[]{:S(2)}, u32[]{:S(2)}) %all-to-all-start.2) | async-done | bytes 2097184 | tf_op jit(solution)/shard_map/all_to_all | solution.py:379
  135.3 0.7 broadcast_in_dim.14
  136.0 5.9 %all-to-all-start.5 = ((f32[64,4,128]{2,1,0:T(4,128)}), f32[64,4,128]{2,1,0:T(4,128)S(1)}, u32[]{:S(2)}, u32[]{:S(2)}) async-start(f32[64,4,128]{2,1,0:T(4,128)} %broadcast_in_dim.14), calls=%async_computation.5 | async-start | bytes 262144 | tf_op jit(solution)/shard_map/all_to_all | solution.py:344
  141.8 1.0 reduce_sum.18
  142.8 10.1 %all-to-all-done.5 = f32[64,4,128]{2,1,0:T(4,128)S(1)} async-done(((f32[64,4,128]{2,1,0:T(4,128)}), f32[64,4,128]{2,1,0:T(4,128)S(1)}, u32[]{:S(2)}, u32[]{:S(2)}) %all-to-all-start.5) | async-done | bytes 131104 | tf_op jit(solution)/shard_map/all_to_all | solution.py:344
  152.9 3.5 %all-to-all-start.3 = ((f32[8,16,1024]{2,1,0:T(8,128)}), f32[8,16,1024]{2,1,0:T(8,128)S(1)}, u32[]{:S(2)}, u32[]{:S(2)}) async-start(f32[8,16,1024]{2,1,0:T(8,128)} %bitcast.10), calls=%async_computation.3 | async-start | bytes 1048576 | tf_op jit(solution)/shard_map/all_to_all | solution.py:381
  156.4 27.8 %factor.1.i0 = f32[2,128,128]{2,1,0:T(8,128)} custom-call(f32[2,128,128]{2,1,0:T(8,128)} %bitcast.19), custom_call_target="tpu_custom_call" | custom-call | flops 268435456 | bytes 1048576 | tf_op jit(solution)/shard_map/factor/pallas_call | solution.py:347
  184.2 2.0 collective-permute-start.10
  186.2 2.0 collective-permute-start.11
  188.2 0.8 collective-permute-start.12
  189.0 3.4 %collective-permute-done.10.i1 = f32[2,128,128]{2,1,0:T(8,128)S(1)} collective-permute-done((f32[2,128,128]{2,1,0:T(8,128)}, f32[2,128,128]{2,1,0:T(8,128)S(1)}, u32[]{:S(2)}, u32[]{:S(2)}) %collective-permute-start.10) | collective-permute-done | bytes 131104 | tf_op jit(solution)/shard_map/ppermute | solution.py:291
  192.4 1.9 collective-permute-done.11.i2
  194.3 1.7 collective-permute-done.12.i3
  196.0 0.0 all-to-all-done.3.cross_ref
  196.0 0.6 copy-done.8
  196.6 0.8 copy-done
  197.4 2.8 %solve.1 = f32[8,16,128]{2,1,0:T(8,128)} custom-call(s32[1]{0:T(128)} %bitcast.col_ref.r_0_, f32[8,16,1024]{2,1,0:T(8,128)} %copy-done, f32[2,128,128]{2,1,0:T(8,128)} %factor.1.i0, f32[2,128,128]{2,1,0:T(8,128)} %copy-done.6, f32[2,128,128]{2,1,0:T(8,128)} %copy-done.7, f32[2,128,128]{2,1,0:T(8,128)} %copy-done.8), custom_call_target="tpu_custom_call" | custom-call | flops 1048576 | bytes 1048576 | tf_op jit(solution)/shard_map/solve/pallas_call | solution.py:383
  (23 shorter events, 0.0 us)
Async XLA Ops:
  3.3 7.6 %collective-permute-start = (bf16[64,1024]{1,0:T(8,128)(2,1)S(1)}, bf16[64,1024]{1,0:T(8,128)(2,1)S(1)}, u32[]{:S(2)}, u32[]{:S(2)}) collective-permute-start(bf16[64,1024]{1,0:T(8,128)(2,1)S(1)} %get-tuple-element.13), channel_id=1, source_target_pairs={{0,1},{4,5},{8,9},{12,13},{16,17},{20,21},{24,25},{28,29},{32,33},... | collective-permute-start | bytes 393224 | tf_op jit(solution)/shard_map/ppermute | solution.py:310
  4.6 6.3 %collective-permute-start.1 = (bf16[64,1024]{1,0:T(8,128)(2,1)S(1)}, bf16[64,1024]{1,0:T(8,128)(2,1)S(1)}, u32[]{:S(2)}, u32[]{:S(2)}) collective-permute-start(bf16[64,1024]{1,0:T(8,128)(2,1)S(1)} %get-tuple-element.12), channel_id=1, source_target_pairs={{0,2},{4,6},{8,10},{12,14},{16,18},{20,22},{24,26},{28,30},{32,34}... | collective-permute-start | bytes 393224 | tf_op jit(solution)/shard_map/ppermute | solution.py:310
  5.3 5.7 %collective-permute-start.2 = (bf16[64,1024]{1,0:T(8,128)(2,1)S(1)}, bf16[64,1024]{1,0:T(8,128)(2,1)S(1)}, u32[]{:S(2)}, u32[]{:S(2)}) collective-permute-start(bf16[64,1024]{1,0:T(8,128)(2,1)S(1)} %get-tuple-element.11), channel_id=1, source_target_pairs={{0,3},{4,7},{8,11},{12,15},{16,19},{20,23},{24,27},{28,31},{32,35}... | collective-permute-start | bytes 393224 | tf_op jit(solution)/shard_map/ppermute | solution.py:310
  10.9 0.7 copy-start.2
  10.9 0.7 copy-start.3
  10.9 0.7 copy-start.4
  44.3 19.3 %all-to-all-start.1 = ((bf16[64,8,128]{2,1,0:T(8,128)(2,1)}), bf16[64,8,128]{2,1,0:T(8,128)(2,1)S(1)}, u32[]{:S(2)}, u32[]{:S(2)}) async-start(bf16[64,8,128]{2,1,0:T(8,128)(2,1)} %get-tuple-element.8), calls=%async_computation.1 | async-start | bytes 262144 | tf_op jit(solution)/shard_map/all_to_all | solution.py:333
  49.3 20.2 %collective-permute-start.3 = (bf16[32,1024]{1,0:T(8,128)(2,1)}, bf16[32,1024]{1,0:T(8,128)(2,1)S(1)}, u32[]{:S(2)}, u32[]{:S(2)}) collective-permute-start(bf16[32,1024]{1,0:T(8,128)(2,1)} %get-tuple-element.7.r_4_.a0), channel_id=1, source_target_pairs={{0,1},{1,2},{2,3},{3,0},{4,5},{5,6},{6,7},{7,4},{8,9},{9,10},{10,1... | collective-permute-start | bytes 196616 | tf_op jit(solution)/shard_map/ppermute | solution.py:291
  53.1 6.5 %copy-start.9 = (bf16[32,1024]{1,0:T(8,128)(2,1)S(1)}, bf16[32,1024]{1,0:T(8,128)(2,1)}, u32[]{:S(2)}) copy-start(bf16[32,1024]{1,0:T(8,128)(2,1)} %get-tuple-element.7.r_4_.a0) | copy-start | bytes 196612
  59.6 16.3 %collective-permute-start.4 = (bf16[32,1024]{1,0:T(8,128)(2,1)S(1)}, bf16[32,1024]{1,0:T(8,128)(2,1)S(1)}, u32[]{:S(2)}, u32[]{:S(2)}) collective-permute-start(bf16[32,1024]{1,0:T(8,128)(2,1)S(1)} %copy-done.9), channel_id=1, source_target_pairs={{0,2},{1,3},{2,0},{3,1},{4,6},{5,7},{6,4},{7,5},{8,10},{9,11},{10,... | collective-permute-start | bytes 196616 | tf_op jit(solution)/shard_map/ppermute | solution.py:291
  61.0 14.9 %collective-permute-start.5 = (bf16[32,1024]{1,0:T(8,128)(2,1)S(1)}, bf16[32,1024]{1,0:T(8,128)(2,1)S(1)}, u32[]{:S(2)}, u32[]{:S(2)}) collective-permute-start(bf16[32,1024]{1,0:T(8,128)(2,1)S(1)} %copy-done.9), channel_id=1, source_target_pairs={{0,3},{1,0},{2,1},{3,2},{4,7},{5,4},{6,5},{7,6},{8,11},{9,8},{10,9... | collective-permute-start | bytes 196616 | tf_op jit(solution)/shard_map/ppermute | solution.py:291
  63.6 0.6 copy-start.1
  66.7 9.3 %collective-permute-start.6 = (bf16[32,1024]{1,0:T(8,128)(2,1)}, bf16[32,1024]{1,0:T(8,128)(2,1)S(1)}, u32[]{:S(2)}, u32[]{:S(2)}) collective-permute-start(bf16[32,1024]{1,0:T(8,128)(2,1)} %pick.1.r_8_), channel_id=1, source_target_pairs={{0,1},{1,2},{2,3},{3,0},{4,5},{5,6},{6,7},{7,4},{8,9},{9,10},{10,1... | collective-permute-start | bytes 196616 | tf_op jit(solution)/shard_map/ppermute | solution.py:291
  67.1 8.9 %collective-permute-start.7 = (bf16[32,1024]{1,0:T(8,128)(2,1)}, bf16[32,1024]{1,0:T(8,128)(2,1)S(1)}, u32[]{:S(2)}, u32[]{:S(2)}) collective-permute-start(bf16[32,1024]{1,0:T(8,128)(2,1)} %pick.1.r_8_), channel_id=1, source_target_pairs={{0,2},{1,3},{2,0},{3,1},{4,6},{5,7},{6,4},{7,5},{8,10},{9,11},{10,... | collective-permute-start | bytes 196616 | tf_op jit(solution)/shard_map/ppermute | solution.py:291
  69.4 6.5 %copy-start.10 = (bf16[32,1024]{1,0:T(8,128)(2,1)}, bf16[32,1024]{1,0:T(8,128)(2,1)S(1)}, u32[]{:S(2)}) copy-start(bf16[32,1024]{1,0:T(8,128)(2,1)S(1)} %collective-permute-done.3.r_5_.a1) | copy-start | bytes 196612
  69.4 6.5 %collective-permute-start.8 = (bf16[32,1024]{1,0:T(8,128)(2,1)}, bf16[32,1024]{1,0:T(8,128)(2,1)S(1)}, u32[]{:S(2)}, u32[]{:S(2)}) collective-permute-start(bf16[32,1024]{1,0:T(8,128)(2,1)} %pick.1.r_8_), channel_id=1, source_target_pairs={{0,3},{1,0},{2,1},{3,2},{4,7},{5,4},{6,5},{7,6},{8,11},{9,8},{10,9... | collective-permute-start | bytes 196616 | tf_op jit(solution)/shard_map/ppermute | solution.py:291
  75.9 0.6 copy-start.11
  75.9 0.6 copy-start.12
  75.9 0.6 copy-start.13
  76.0 0.7 copy-start.14
  76.0 0.7 copy-start.15
  81.3 17.2 %collective-permute-start.9 = (f32[512,1024]{1,0:T(8,128)}, f32[512,1024]{1,0:T(8,128)S(1)}, u32[]{:S(2)}, u32[]{:S(2)}) collective-permute-start(f32[512,1024]{1,0:T(8,128)} %cross0.1), channel_id=1, source_target_pairs={{0,4},{4,0},{8,12},{12,8},{16,20},{20,16},{24,28},{28,24},{32,36},... | collective-permute-start | bytes 6291464 | tf_op jit(solution)/shard_map/ppermute | solution.py:371
  85.0 19.9 %all-to-all-start.4 = ((f32[64,4,128]{2,1,0:T(4,128)}), f32[64,4,128]{2,1,0:T(4,128)S(1)}, u32[]{:S(2)}, u32[]{:S(2)}) async-start(f32[64,4,128]{2,1,0:T(4,128)} %bitcast.11), calls=%async_computation.4 | async-start | bytes 262144 | tf_op jit(solution)/shard_map/all_to_all | solution.py:342
  104.8 30.5 %all-to-all-start.2 = ((f32[4,128,1024]{2,1,0:T(8,128)}), f32[4,128,1024]{2,1,0:T(8,128)S(1)}, u32[]{:S(2)}, u32[]{:S(2)}) async-start(f32[4,128,1024]{2,1,0:T(8,128)} %bitcast.9), calls=%async_computation.2 | async-start | bytes 4194304 | tf_op jit(solution)/shard_map/all_to_all | solution.py:379
  136.0 16.9 %all-to-all-start.5 = ((f32[64,4,128]{2,1,0:T(4,128)}), f32[64,4,128]{2,1,0:T(4,128)S(1)}, u32[]{:S(2)}, u32[]{:S(2)}) async-start(f32[64,4,128]{2,1,0:T(4,128)} %broadcast_in_dim.14), calls=%async_computation.5 | async-start | bytes 262144 | tf_op jit(solution)/shard_map/all_to_all | solution.py:344
  152.9 3.5 %copy-start.5 = (f32[64,4,128]{2,1,0:T(4,128)}, f32[64,4,128]{2,1,0:T(4,128)S(1)}, u32[]{:S(2)}) copy-start(f32[64,4,128]{2,1,0:T(4,128)S(1)} %all-to-all-done.5) | copy-start | bytes 393220
  152.9 43.1 %all-to-all-start.3 = ((f32[8,16,1024]{2,1,0:T(8,128)}), f32[8,16,1024]{2,1,0:T(8,128)S(1)}, u32[]{:S(2)}, u32[]{:S(2)}) async-start(f32[8,16,1024]{2,1,0:T(8,128)} %bitcast.10), calls=%async_computation.3 | async-start | bytes 1048576 | tf_op jit(solution)/shard_map/all_to_all | solution.py:381
  184.2 8.2 %collective-permute-start.10 = (f32[2,128,128]{2,1,0:T(8,128)}, f32[2,128,128]{2,1,0:T(8,128)S(1)}, u32[]{:S(2)}, u32[]{:S(2)}) collective-permute-start(f32[2,128,128]{2,1,0:T(8,128)} %factor.1.i0), channel_id=1, source_target_pairs={{0,1},{1,2},{2,3},{3,0},{4,5},{5,6},{6,7},{7,4},{8,9},{9,10},{10,1... | collective-permute-start | bytes 393224 | tf_op jit(solution)/shard_map/ppermute | solution.py:291
  186.2 8.1 %collective-permute-start.11 = (f32[2,128,128]{2,1,0:T(8,128)}, f32[2,128,128]{2,1,0:T(8,128)S(1)}, u32[]{:S(2)}, u32[]{:S(2)}) collective-permute-start(f32[2,128,128]{2,1,0:T(8,128)} %factor.1.i0), channel_id=1, source_target_pairs={{0,2},{1,3},{2,0},{3,1},{4,6},{5,7},{6,4},{7,5},{8,10},{9,11},{10,... | collective-permute-start | bytes 393224 | tf_op jit(solution)/shard_map/ppermute | solution.py:291
  188.2 7.8 %collective-permute-start.12 = (f32[2,128,128]{2,1,0:T(8,128)}, f32[2,128,128]{2,1,0:T(8,128)S(1)}, u32[]{:S(2)}, u32[]{:S(2)}) collective-permute-start(f32[2,128,128]{2,1,0:T(8,128)} %factor.1.i0), channel_id=1, source_target_pairs={{0,3},{1,0},{2,1},{3,2},{4,7},{5,4},{6,5},{7,6},{8,11},{9,8},{10,9... | collective-permute-start | bytes 393224 | tf_op jit(solution)/shard_map/ppermute | solution.py:291
  192.4 3.6 %copy-start.6 = (f32[2,128,128]{2,1,0:T(8,128)}, f32[2,128,128]{2,1,0:T(8,128)S(1)}, u32[]{:S(2)}) copy-start(f32[2,128,128]{2,1,0:T(8,128)S(1)} %collective-permute-done.10.i1) | copy-start | bytes 393220
  194.3 1.7 copy-start.7
  196.0 0.6 copy-start.8
  196.6 0.8 copy-start

commit v2 on v1

--- a/solution.py
+++ b/solution.py
@@ -7,6 +7,7 @@
 
 NB = 128
 CORES = 2
+LIMIT = 30 << 20
 X = 4
 BF = jnp.bfloat16
 F32 = jnp.float32
@@ -40,23 +41,24 @@
         scratch_shapes=scratch,
         cost_estimate=pl.CostEstimate(flops=flops, bytes_accessed=1 << 20, transcendentals=0),
         name=name,
+        compiler_params=pltpu.CompilerParams(vmem_limit_bytes=LIMIT),
     )
 
 
 SMEM = pl.BlockSpec(memory_space=pltpu.SMEM)
 
 
-def lead_kernel(child_ref, front_ref, heights_ref, out_ref):
+def lead_kernel(child_ref, front_ref, heights_ref, *out_refs):
     eye = onehot(iota((NB, NB), 0) == iota((NB, NB), 1))
-    quarter = out_ref.shape[1] // 2
+    quarter = out_refs[0].shape[0] // 2
     child = dot(eye, child_ref[...], 1, 1).astype(BF)
-    for c in range(out_ref.shape[0]):
-        out_ref[c, :quarter] = child[c * quarter : (c + 1) * quarter]
+    for c, out_ref in enumerate(out_refs):
+        out_ref[:quarter] = child[c * quarter : (c + 1) * quarter]
     for f in range(front_ref.shape[0]):
         own = dot(eye, front_ref[f], 1, 1)
         own = jnp.where(iota(own.shape, 1) < heights_ref[0, f], own, 0.0).astype(BF)
-        for c in range(out_ref.shape[0]):
-            out_ref[c, quarter:, f * NB : (f + 1) * NB] = own[c * quarter : (c + 1) * quarter]
+        for c, out_ref in enumerate(out_refs):
+            out_ref[quarter:, f * NB : (f + 1) * NB] = own[c * quarter : (c + 1) * quarter]
 
 
 def index_kernel(peers, capacity, groups, dest_ref, key_ref):
@@ -79,7 +81,7 @@
 
 
 def quarter_of(col, parts, low, high):
-    base = parts[0][0, low:high].astype(F32)
+    base = parts[0][low:high].astype(F32)
     total = jnp.where(col == 0, base, jnp.zeros_like(base))
     for part in parts[1:]:
         total = total + part[low:high].astype(F32)
@@ -161,8 +163,8 @@
     out_ref[...] = total.astype(BF)
 
 
-def turn_kernel(core_ref, child_ref, front_ref, out_ref):
-    halves, xs, zs, run, _ = out_ref.shape
+def turn_kernel(core_ref, child_ref, front_ref, *out_refs):
+    xs, zs, run, _ = out_refs[0].shape
     row, column = iota((NB, NB), 0), iota((NB, NB), 1)
     half = row // (xs * run)
     core = jnp.where(half == 0, 1 - core_ref[0], core_ref[0])
@@ -175,10 +177,10 @@
             for f in range(front_ref.shape[0])
         ]
         turned = jnp.concatenate(own + [turned], axis=1)
-        for h in range(halves):
+        for h, out_ref in enumerate(out_refs):
             for x in range(xs):
                 low = (h * xs + x) * run
-                out_ref[h, x, z] = turned[low : low + run]
+                out_ref[x, z] = turned[low : low + run]
 
 
 def ring_into(col, parts, whole):
@@ -223,40 +225,44 @@
 
 def gram_kernel(col_ref, a0, a1, a2, a3, out_ref, panel_ref):
     ring_into(col_ref[0], (a0, a1, a2, a3), panel_ref)
-    panel = panel_ref[...].reshape(NB, panel_ref.shape[2])
-    for f in range(out_ref.shape[0] // NB):
-        block = panel[:, f * NB : (f + 1) * NB]
+    share = out_ref.shape[0]
+    for f in range(share // NB):
+        low = pl.multiple_of(col_ref[0] * share + f * NB, NB)
+        block = panel_ref[:, :, pl.ds(low, NB)].reshape(NB, NB)
         out_ref[f * NB : (f + 1) * NB] = dot(block, block, 1, 1)
 
 
 def factor_kernel(gram_ref, out_ref, a_ref):
     n = gram_ref.shape[0]
-    row, column = iota((NB, NB), 0), iota((NB, NB), 1)
+    step = 8
+    sub, lane = iota((step, NB), 0), iota((step, NB), 1)
     for f in range(n):
         a_ref[f] = gram_ref[f]
-        out_ref[f] = jnp.where(row == column, 1.0, 0.0)
-
-    def block(t, carry):
-        for j in range(8):
-            for f in range(n):
-                a = a_ref[f]
-                pivot_rows = a_ref[f, pl.ds(t * 8, 8), :]
-                pivot_row = pivot_rows[j : j + 1]
-                inverse_rows = out_ref[f, pl.ds(t * 8, 8), :]
-                inverse_row = inverse_rows[j : j + 1]
-                factor = a[:, j : j + 1] * (1.0 / pivot_row[:, j : j + 1])
-                factor = jnp.where(row[:, :1] > t * 8 + j, factor, 0.0)
-                a_ref[f] = a - factor * pivot_row
-                out_ref[f] = out_ref[f] - factor * inverse_row
+        out_ref[f] = jnp.where(iota((NB, NB), 0) == iota((NB, NB), 1), 1.0, 0.0)
+    for t in range(NB // step):
+        low, high = t * step, (t + 1) * step
         for f in range(n):
-            rows = a_ref[f, pl.ds(t * 8, 8), :]
-            eye = iota((8, NB), 0) == iota((8, NB), 1)
-            d = jnp.sum(jnp.where(eye, rows, 0.0), axis=1, keepdims=True)
-            out_ref[f, pl.ds(t * 8, 8), :] = out_ref[f, pl.ds(t * 8, 8), :] * lax.rsqrt(d)
-            a_ref[f] = pltpu.roll(a_ref[f], NB - 8, 1)
-        return carry
-
-    lax.fori_loop(0, NB // 8, block, 0)
+            top, inverse = a_ref[f, low:high, :], out_ref[f, low:high, :]
+            diagonal = jnp.zeros((step, 1), F32)
+            for j in range(step):
+                column = top[:, low + j : low + j + 1]
+                pivot = column[j : j + 1]
+                factor = jnp.where(sub[:, :1] > j, column / pivot, 0.0)
+                diagonal = jnp.where(sub[:, :1] == j, pivot, diagonal)
+                top = top - factor * top[j : j + 1]
+                inverse = inverse - factor * inverse[j : j + 1]
+            scale = lax.rsqrt(diagonal)
+            inverse = inverse * scale
+            out_ref[f, low:high, :] = inverse
+            if high < NB:
+                top = jnp.where(lane >= high, top * scale, 0.0)
+                change = dot(
+                    top,
+                    jnp.concatenate([top, inverse], axis=1), 0, 0,
+                    precision=lax.Precision.HIGHEST,
+                )
+                a_ref[f, high:, :] = a_ref[f, high:, :] - change[high:, :NB]
+                out_ref[f, high:, :] = out_ref[f, high:, :] - change[high:, NB:]
 
 
 def solve_kernel(col_ref, cross_ref, i0, i1, i2, i3, out_ref, inverse_ref):
@@ -298,16 +304,16 @@
     lead = pl.pallas_call(
         lead_kernel,
         grid=(1,),
-        out_shape=sds((cols, 2 * quarter, count), BF),
+        out_shape=[sds((2 * quarter, count), BF)] * cols,
         in_specs=[
             pl.BlockSpec((count, NB), lambda i: (0, 0)),
             pl.BlockSpec((fronts, height_cap, NB), lambda i: (0, 0, 0)),
             SMEM,
         ],
-        out_specs=pl.BlockSpec((cols, 2 * quarter, count), lambda i: (0, 0, 0)),
+        out_specs=[pl.BlockSpec((2 * quarter, count), lambda i: (0, 0))] * cols,
         name="lead",
     )(child_rows, front_rows, heights)
-    parts = [lead] + [lax.ppermute(lead[d], "cols", [(0, d)]) for d in range(1, cols)]
+    parts = [lead[0]] + [lax.ppermute(lead[d], "cols", [(0, d)]) for d in range(1, cols)]
 
     key = call(
         lambda *r: index_kernel(peers, capacity, cols, *r), sds((1, count), I32), vmem(1),
@@ -316,13 +322,14 @@
     send = call(
         pack_kernel, sds((peers, 2 * per, NB), BF), [SMEM, SMEM] + vmem(6), name="pack"
     )(col, parent_ids, key, slot, *parts)
-    got = lax.all_to_all(send, "rows", 0, 0, tiled=True)
 
     rows = call(
-        turn_kernel, sds((CORES, X, zs, run, targets + count), BF), [SMEM] + vmem(2),
+        turn_kernel, [sds((X, zs, run, targets + count), BF)] * CORES, [SMEM] + vmem(2),
         flops=1 << 29, name="turn",
     )(core, child_rows, front_rows)
 
+    got = lax.all_to_all(send, "rows", 0, 0, tiled=True)
+    got, rows = lax.optimization_barrier((got, rows))
     panel, back = call(
         panel_kernel,
         (sds((quarter, targets), BF), sds((peers, per, NB), BF)),
@@ -334,13 +341,18 @@
     panels = spread(panel)
 
     whole = [pltpu.VMEM((cols, quarter, targets), BF)]
-    gram = call(gram_kernel, sds((fronts * NB, NB), F32), [SMEM] + vmem(4), whole, name="gram")(
+    share = fronts // cols * NB
+    gram = call(gram_kernel, sds((share, NB), F32), [SMEM] + vmem(4), whole, name="gram")(
         col, *panels
     )
-    share = fronts // cols * NB
-    mine = lax.dynamic_slice_in_dim(gram, col[0] * share, share, 0)
-    sums = lax.all_to_all(mine.reshape(peers, share // peers, NB), "rows", 0, 0, tiled=True)
+    returned, gram = lax.optimization_barrier((returned, gram))
+    sums = lax.all_to_all(gram.reshape(peers, share // peers, NB), "rows", 0, 0, tiled=True)
     sums = jnp.sum(sums, axis=0)
+
+    picked = call(pick_kernel, sds((quarter, count), BF), vmem(2), name="pick")(key, returned)
+    pickeds = spread(picked)
+    pickeds, sums = lax.optimization_barrier((pickeds, sums))
+
     sums = lax.all_to_all(
         jnp.broadcast_to(sums[None], (peers, share // peers, NB)), "rows", 0, 0, tiled=True
     )
@@ -348,10 +360,6 @@
         factor_kernel, sds((fronts // cols, NB, NB), F32), vmem(1),
         [pltpu.VMEM((fronts // cols, NB, NB), F32)], flops=1 << 28, name="factor",
     )(sums.reshape(fronts // cols, NB, NB))
-    inverses = spread(inverse)
-
-    picked = call(pick_kernel, sds((quarter, count), BF), vmem(2), name="pick")(key, returned)
-    pickeds = spread(picked)
 
     halves = []
     for h in range(CORES):
@@ -377,6 +385,8 @@
     over_x = [[at(z, x, c) for x in range(X)] for z in range(zs) for c in range(CORES)]
     over_z = [[at(z, x, c) for z in range(zs)] for x in range(X) for c in range(CORES)]
     chip = lax.all_to_all(chip, "rows", 0, 0, axis_index_groups=over_x, tiled=True)
+    chip, inverse = lax.optimization_barrier((chip, inverse))
+    inverses = spread(inverse)
     chip = jnp.sum(chip, axis=0).reshape(zs, run, targets)
     chip = lax.all_to_all(chip, "rows", 0, 0, axis_index_groups=over_z, tiled=True)
 

time: 201 us -> 161 us (0.80)
  Pallas kernels: 62.5 us -> 36 us
  blocking collectives: 24.9 us -> 0 us
  starting transfers between devices: 46.3 us -> 63.6 us
  local copies, waits for them, and re-layouts: 11.6 us -> 7.59 us
  waiting for transfers between devices: 50.3 us -> 46.6 us
    all_to_all x1 -> x0, blocking collectives: 24.9 us -> none  [on_device(): got = lax.all_to_all(send, 'rows', 0, 0, tiled=True)]
    all_to_all x1, waiting for transfers between devices: 26.8 us -> 10.4 us  [on_device(): lax.all_to_all(chip, 'rows', 0, 0, axis_index_groups=over_x, tiled=True)]
    all_to_all x1 -> x2, starting transfers between devices: 8.81 us -> 21.9 us  [the longest x1 11.9 us: on_device(): got = lax.all_to_all(send, 'rows', 0, 0, tiled=True)]
    pallas_call x1, Pallas kernels: 27.8 us -> 16.5 us  [on_device(): call(factor_kernel, sds((fronts // cols, NB, NB), F32), vmem(1), [pltpu.V...]
    all_to_all x1 -> x2, waiting for transfers between devices: 3.02 us -> 11 us  [the longest x1 6.35 us: on_device(): got = lax.all_to_all(send, 'rows', 0, 0, tiled=True)]
    all_to_all x1, waiting for transfers between devices: 0.01 us -> 7.77 us  [on_device(): lax.all_to_all(chip, 'rows', 0, 0, axis_index_groups=over_z, tiled=True)]
    squeeze x2 -> x0, local copies, waits for them, and re-layouts: 5.89 us -> none  [the longest x1 4.84 us: on_device(): rows[h]]
    pallas_call x3, Pallas kernels: 10.8 us -> 5.42 us  [the longest x1 2.35 us: on_device(): pl.pallas_call(lead_kernel, grid=(1,), out_shape=[sds((2 * quarter, count...]
  transfers between devices with their start and end apart: 18 -> 19, of which waited for: 7 -> 12; matrix products, arithmetic and copies ran while one was open for 5% -> 3% of each run, Pallas kernels for 23% -> 14%
where the time goes in v2:
time: 161 us; the launch traced here: 159 us
  starting transfers between devices  63.6 us (40%)
  waiting for transfers between devices  46.6 us (29%)
  Pallas kernels  36 us (22%)
  local copies, waits for them, and re-layouts  7.59 us (5%)
  other arithmetic  4.39 us (3%)
    ppermute x9, starting transfers between devices, spread(): lax.ppermute(value, 'cols', [(i, (i + d) % cols) for i in range(cols)])  18.1 us
    pallas_call x1, Pallas kernels, on_device(): call(factor_kernel, sds((fronts // cols, NB, NB), F32), vmem(1), [pltpu.V...  16.5 us
    all_to_all x1, starting transfers between devices, on_device(): got = lax.all_to_all(send, 'rows', 0, 0, tiled=True)  11.9 us
    all_to_all x1, waiting for transfers between devices, on_device(): lax.all_to_all(chip, 'rows', 0, 0, axis_index_groups=over_x, tiled=True)  10.4 us
    all_to_all x1, starting transfers between devices, on_device(): lax.all_to_all(gram.reshape(peers, share // peers, NB), 'rows', 0, 0, til...  10 us
    all_to_all x1, starting transfers between devices, on_device(): lax.all_to_all(jnp.broadcast_to(sums[None], (peers, share // peers, NB)),...  8.83 us
    all_to_all x1, waiting for transfers between devices, on_device(): lax.all_to_all(chip, 'rows', 0, 0, axis_index_groups=over_z, tiled=True)  7.77 us
    unnamed x24, local copies, waits for them, and re-layouts  6.91 us
  transfers between devices with their start and end apart: 19, of which 12 were waited for; matrix products, arithmetic and copies ran while one was open for 3% of the time, Pallas kernels for 14%

profile of v2, /device:TPU:8, one launch (start us, length us, event | category | flops | bytes accessed | tf_op | source)
XLA Modules:
  0.0 158.5 jit_solution(14007964374836924154)
XLA Ops:
  0.0 0.0 copy-start.4
  0.0 2.4 %lead.1 = (bf16[64,1024]{1,0:T(8,128)(2,1)}, bf16[64,1024]{1,0:T(8,128)(2,1)}, bf16[64,1024]{1,0:T(8,128)(2,1)}, bf16[64,1024]{1,0:T(8,128)(2,1)}) custom-call(bf16[1024,1024]{1,0:T(8,128)(2,1)} %child_ref.3, bf16[8,128,1024]{2,1,0:T(8,128)(2,1)} %front_ref.3, s32[1,8]{1,0:T(1,128)} %r_2_.3), custom_call_target="tpu_custom_call" | custom-call | tf_op jit(solution)/shard_map/lead/pallas_call | solution.py:304
  2.4 1.3 collective-permute-start
  3.7 0.7 collective-permute-start.1
  4.3 0.7 collective-permute-start.2
  5.0 0.2 index.1.key_ref
  5.3 4.9 %collective-permute-done.p1 = bf16[64,1024]{1,0:T(8,128)(2,1)S(1)} collective-permute-done((bf16[64,1024]{1,0:T(8,128)(2,1)}, bf16[64,1024]{1,0:T(8,128)(2,1)S(1)}, u32[]{:S(2)}, u32[]{:S(2)}) %collective-permute-start) | collective-permute-done | bytes 131104 | tf_op jit(solution)/shard_map/ppermute | solution.py:316
  10.2 0.0 collective-permute-done.1.p2
  10.2 0.0 collective-permute-done.2.p3
  10.2 0.9 copy-done.2
  11.1 2.5 %pack.1 = bf16[64,16,128]{2,1,0:T(8,128)(2,1)} custom-call(s32[1]{0:T(128)} %bitcast.col_ref.r_0_, s32[16]{0:T(128)S(1)} %copy-done.6, s32[1,1024]{1,0:T(1,128)S(1)} %index.1.key_ref, s32[1,1024]{1,0:T(1,128)S(1)} %bitcast.10, bf16[64,1024]{1,0:T(8,128)(2,1)S(1)} %copy-done.2, bf16[64,1024]{1,0:T(8,128)(2,1)S(1)} %collective-permute-done.p1, ...), custom_call_target="tpu_custom_call" | custom-call | flops 1048576 | bytes 1048576 | tf_op jit(solution)/shard_map/pack/pallas_call | solution.py:322
  13.6 11.9 %all-to-all-start = ((bf16[64,16,128]{2,1,0:T(8,128)(2,1)}), bf16[64,16,128]{2,1,0:T(8,128)(2,1)S(1)}, u32[]{:S(2)}, u32[]{:S(2)}) async-start(bf16[64,16,128]{2,1,0:T(8,128)(2,1)} %pack.1), calls=%async_computation | async-start | bytes 524288 | tf_op jit(solution)/shard_map/all_to_all | solution.py:331
  25.6 0.0 copy-start.1
  25.6 1.6 copy-done.1
  27.2 2.2 %turn.1 = (bf16[4,8,16,2048]{3,2,1,0:T(8,128)(2,1)S(1)}, bf16[4,8,16,2048]{3,2,1,0:T(8,128)(2,1)S(1)}) custom-call(s32[1]{0:T(128)} %bitcast.3.core_ref, bf16[1024,1024]{1,0:T(8,128)(2,1)S(1)} %copy-done, bf16[8,128,1024]{2,1,0:T(8,128)(2,1)S(1)} %copy-done.1), custom_call_target="tpu_custom_call" | custom-call | flops 536870912 | bytes 1048576 | tf_op jit(solution)/shard_map/turn/pallas_call | solution.py:326
  29.4 0.0 copy-start.8
  29.4 1.3 copy-done.8
  30.8 1.3 copy-done.10
  32.1 6.4 %all-to-all-done.got_ref = bf16[64,16,128]{2,1,0:T(8,128)(2,1)S(1)} async-done(((bf16[64,16,128]{2,1,0:T(8,128)(2,1)}), bf16[64,16,128]{2,1,0:T(8,128)(2,1)S(1)}, u32[]{:S(2)}, u32[]{:S(2)}) %all-to-all-start) | async-done | bytes 262176 | tf_op jit(solution)/shard_map/all_to_all | solution.py:331
  38.5 3.3 %panel.1 = (bf16[32,1024]{1,0:T(8,128)(2,1)S(1)}, bf16[64,8,128]{2,1,0:T(8,128)(2,1)}) custom-call(s32[1]{0:T(128)} %bitcast.col_ref.r_0_, bf16[64,16,128]{2,1,0:T(8,128)(2,1)S(1)} %all-to-all-done.got_ref, bf16[64,1024]{1,0:T(8,128)(2,1)S(1)} %copy-done.3, bf16[64,1024]{1,0:T(8,128)(2,1)S(1)} %collective-permute-done.p1, ...), custom_call_target="tpu_custom_call" | custom-call | flops 1048576 | bytes 1048576 | tf_op jit(solution)/shard_map/panel/pallas_call | solution.py:333
  41.8 5.0 %all-to-all-start.1 = ((bf16[64,8,128]{2,1,0:T(8,128)(2,1)}), bf16[64,8,128]{2,1,0:T(8,128)(2,1)S(1)}, u32[]{:S(2)}, u32[]{:S(2)}) async-start(bf16[64,8,128]{2,1,0:T(8,128)(2,1)} %get-tuple-element.34), calls=%async_computation.1 | async-start | bytes 262144 | tf_op jit(solution)/shard_map/all_to_all | solution.py:340
  46.8 2.8 %collective-permute-start.5 = (bf16[32,1024]{1,0:T(8,128)(2,1)S(1)}, bf16[32,1024]{1,0:T(8,128)(2,1)S(1)}, u32[]{:S(2)}, u32[]{:S(2)}) collective-permute-start(bf16[32,1024]{1,0:T(8,128)(2,1)S(1)} %get-tuple-element.33.a0.r_4_), channel_id=1, source_target_pairs={{0,3},{1,0},{2,1},{3,2},{4,7},{5,4},{6,5},{7,6},{8,11},{9,8},{10,9... | collective-permute-start | bytes 196616 | tf_op jit(solution)/shard_map/ppermute | solution.py:297
  49.6 2.5 %collective-permute-start.4 = (bf16[32,1024]{1,0:T(8,128)(2,1)S(1)}, bf16[32,1024]{1,0:T(8,128)(2,1)S(1)}, u32[]{:S(2)}, u32[]{:S(2)}) collective-permute-start(bf16[32,1024]{1,0:T(8,128)(2,1)S(1)} %get-tuple-element.33.a0.r_4_), channel_id=1, source_target_pairs={{0,2},{1,3},{2,0},{3,1},{4,6},{5,7},{6,4},{7,5},{8,10},{9,11},{10,... | collective-permute-start | bytes 196616 | tf_op jit(solution)/shard_map/ppermute | solution.py:297
  52.1 2.5 %collective-permute-start.3 = (bf16[32,1024]{1,0:T(8,128)(2,1)S(1)}, bf16[32,1024]{1,0:T(8,128)(2,1)S(1)}, u32[]{:S(2)}, u32[]{:S(2)}) collective-permute-start(bf16[32,1024]{1,0:T(8,128)(2,1)S(1)} %get-tuple-element.33.a0.r_4_), channel_id=1, source_target_pairs={{0,1},{1,2},{2,3},{3,0},{4,5},{5,6},{6,7},{7,4},{8,9},{9,10},{10,1... | collective-permute-start | bytes 196616 | tf_op jit(solution)/shard_map/ppermute | solution.py:297
  54.6 0.0 collective-permute-done.5.a3.r_7_
  54.6 1.1 collective-permute-done.4.a2.r_6_
  55.7 0.9 collective-permute-done.3.a1.r_5_
  56.6 0.8 gram.1
  57.4 0.4 all-to-all-done.1.got_ref
  57.8 10.0 %all-to-all-start.2 = ((f32[64,4,128]{2,1,0:T(4,128)}), f32[64,4,128]{2,1,0:T(4,128)S(1)}, u32[]{:S(2)}, u32[]{:S(2)}) async-start(f32[64,4,128]{2,1,0:T(4,128)} %bitcast.4), calls=%async_computation.2 | async-start | bytes 262144 | tf_op jit(solution)/shard_map/all_to_all | solution.py:349
  67.8 0.9 pick.1.r_8_
  68.7 3.2 %collective-permute-start.8 = (bf16[32,1024]{1,0:T(8,128)(2,1)S(1)}, bf16[32,1024]{1,0:T(8,128)(2,1)S(1)}, u32[]{:S(2)}, u32[]{:S(2)}) collective-permute-start(bf16[32,1024]{1,0:T(8,128)(2,1)S(1)} %pick.1.r_8_), channel_id=1, source_target_pairs={{0,3},{1,0},{2,1},{3,2},{4,7},{5,4},{6,5},{7,6},{8,11},{9,8},{10,9... | collective-permute-start | bytes 196616 | tf_op jit(solution)/shard_map/ppermute | solution.py:297
  71.9 0.7 collective-permute-start.7
  72.6 1.6 %collective-permute-start.6 = (bf16[32,1024]{1,0:T(8,128)(2,1)S(1)}, bf16[32,1024]{1,0:T(8,128)(2,1)S(1)}, u32[]{:S(2)}, u32[]{:S(2)}) collective-permute-start(bf16[32,1024]{1,0:T(8,128)(2,1)S(1)} %pick.1.r_8_), channel_id=1, source_target_pairs={{0,1},{1,2},{2,3},{3,0},{4,5},{5,6},{6,7},{7,4},{8,9},{9,10},{10,1... | collective-permute-start | bytes 196616 | tf_op jit(solution)/shard_map/ppermute | solution.py:297
  74.2 4.7 %all-to-all-done.2 = f32[64,4,128]{2,1,0:T(4,128)S(1)} async-done(((f32[64,4,128]{2,1,0:T(4,128)}), f32[64,4,128]{2,1,0:T(4,128)S(1)}, u32[]{:S(2)}, u32[]{:S(2)}) %all-to-all-start.2) | async-done | bytes 131104 | tf_op jit(solution)/shard_map/all_to_all | solution.py:349
  78.8 0.1 reduce_sum.18
  78.9 0.0 collective-permute-done.8.r_11_
  78.9 0.0 collective-permute-done.7.r_10_
  78.9 0.0 collective-permute-done.6.r_9_
  79.0 0.0 copy-done.7
  79.0 0.0 copy-start.11
  79.0 1.7 %copy-done.11 = bf16[4,8,16,2048]{3,2,1,0:T(8,128)(2,1)S(1)} copy-done((bf16[4,8,16,2048]{3,2,1,0:T(8,128)(2,1)S(1)}, bf16[4,8,16,2048]{3,2,1,0:T(8,128)(2,1)}, u32[]{:S(2)}) %copy-start.11) | copy-done | bytes 2097176
  80.7 3.5 %cross0.1 = f32[512,1024]{1,0:T(8,128)} custom-call(s32[1]{0:T(128)} %bitcast.col_ref.r_0_, s32[16]{0:T(128)S(1)} %copy-done.6, s32[1,8]{1,0:T(1,128)S(1)} %copy-done.7, bf16[4,8,16,2048]{3,2,1,0:T(8,128)(2,1)S(1)} %copy-done.11, bf16[32,1024]{1,0:T(8,128)(2,1)S(1)} %get-tuple-element.33.a0.r_4_, bf16[32,1024]{1,0:T(8,128)(2,1)S(1)} %collective-permute-done.3.a1.r_5_, ...), custom_call_target="tpu_custom_call" | custom-call | flops 2147483648 | bytes 1048576 | tf_op jit(solution)/shard_map/cross0/pallas_call | solution.py:367
  84.2 0.1 collective-permute-start.9
  84.3 0.7 broadcast_in_dim.14
  85.0 8.8 %all-to-all-start.4 = ((f32[64,4,128]{2,1,0:T(4,128)}), f32[64,4,128]{2,1,0:T(4,128)S(1)}, u32[]{:S(2)}, u32[]{:S(2)}) async-start(f32[64,4,128]{2,1,0:T(4,128)} %broadcast_in_dim.14), calls=%async_computation.4 | async-start | bytes 262144 | tf_op jit(solution)/shard_map/all_to_all | solution.py:356
  93.8 0.0 copy-done.9
  93.8 2.1 %cross1.1 = f32[512,1024]{1,0:T(8,128)S(1)} custom-call(s32[1]{0:T(128)} %bitcast.col_ref.r_0_, s32[16]{0:T(128)S(1)} %copy-done.6, s32[1,8]{1,0:T(1,128)S(1)} %copy-done.7, bf16[4,8,16,2048]{3,2,1,0:T(8,128)(2,1)S(1)} %copy-done.9, bf16[32,1024]{1,0:T(8,128)(2,1)S(1)} %get-tuple-element.33.a0.r_4_, bf16[32,1024]{1,0:T(8,128)(2,1)S(1)} %collective-permute-done.3.a1.r_5_, ...), custom_call_target="tpu_custom_call" | custom-call | flops 2147483648 | bytes 1048576 | tf_op jit(solution)/shard_map/cross1/pallas_call | solution.py:367
  96.0 0.0 collective-permute-done.9
  96.0 3.3 %add.8 = f32[512,1024]{1,0:T(8,128)} add(f32[512,1024]{1,0:T(8,128)S(1)} %cross1.1, f32[512,1024]{1,0:T(8,128)} %collective-permute-done.9) | non-fusion elementwise | flops 524288 | bytes 6291456 | tf_op jit(solution)/shard_map/add | solution.py:380
  99.3 5.6 %all-to-all-done.4 = f32[64,4,128]{2,1,0:T(4,128)S(1)} async-done(((f32[64,4,128]{2,1,0:T(4,128)}), f32[64,4,128]{2,1,0:T(4,128)S(1)}, u32[]{:S(2)}, u32[]{:S(2)}) %all-to-all-start.4) | async-done | bytes 131104 | tf_op jit(solution)/shard_map/all_to_all | solution.py:356
  104.9 3.6 %all-to-all-start.3 = ((f32[4,128,1024]{2,1,0:T(8,128)}), f32[4,128,1024]{2,1,0:T(8,128)S(1)}, u32[]{:S(2)}, u32[]{:S(2)}) async-start(f32[4,128,1024]{2,1,0:T(8,128)} %bitcast.5), calls=%async_computation.3 | async-start | bytes 4194304 | tf_op jit(solution)/shard_map/all_to_all | solution.py:387
  108.5 16.5 %factor.1.i0 = f32[2,128,128]{2,1,0:T(8,128)S(1)} custom-call(f32[2,128,128]{2,1,0:T(8,128)S(1)} %bitcast.9), custom_call_target="tpu_custom_call" | custom-call | flops 268435456 | bytes 1048576 | tf_op jit(solution)/shard_map/factor/pallas_call | solution.py:359
  124.9 10.4 %all-to-all-done.3 = f32[4,128,1024]{2,1,0:T(8,128)S(1)} async-done(((f32[4,128,1024]{2,1,0:T(8,128)}), f32[4,128,1024]{2,1,0:T(8,128)S(1)}, u32[]{:S(2)}, u32[]{:S(2)}) %all-to-all-start.3) | async-done | bytes 2097184 | tf_op jit(solution)/shard_map/all_to_all | solution.py:387
  135.3 1.0 reduce_sum.19
  136.3 3.5 %all-to-all-start.5 = ((f32[8,16,1024]{2,1,0:T(8,128)}), f32[8,16,1024]{2,1,0:T(8,128)S(1)}, u32[]{:S(2)}, u32[]{:S(2)}) async-start(f32[8,16,1024]{2,1,0:T(8,128)} %bitcast.7), calls=%async_computation.5 | async-start | bytes 1048576 | tf_op jit(solution)/shard_map/all_to_all | solution.py:391
  139.8 1.9 %collective-permute-start.12 = (f32[2,128,128]{2,1,0:T(8,128)S(1)}, f32[2,128,128]{2,1,0:T(8,128)S(1)}, u32[]{:S(2)}, u32[]{:S(2)}) collective-permute-start(f32[2,128,128]{2,1,0:T(8,128)S(1)} %factor.1.i0), channel_id=1, source_target_pairs={{0,3},{1,0},{2,1},{3,2},{4,7},{5,4},{6,5},{7,6},{8,11},{9,8},{10,9... | collective-permute-start | bytes 393224 | tf_op jit(solution)/shard_map/ppermute | solution.py:297
  141.7 0.4 collective-permute-start.11
  142.2 2.4 %collective-permute-start.10 = (f32[2,128,128]{2,1,0:T(8,128)S(1)}, f32[2,128,128]{2,1,0:T(8,128)S(1)}, u32[]{:S(2)}, u32[]{:S(2)}) collective-permute-start(f32[2,128,128]{2,1,0:T(8,128)S(1)} %factor.1.i0), channel_id=1, source_target_pairs={{0,1},{1,2},{2,3},{3,0},{4,5},{5,6},{6,7},{7,4},{8,9},{9,10},{10,1... | collective-permute-start | bytes 393224 | tf_op jit(solution)/shard_map/ppermute | solution.py:297
  144.5 0.8 collective-permute-done.12.i3
  145.3 2.9 %collective-permute-done.11.i2 = f32[2,128,128]{2,1,0:T(8,128)S(1)} collective-permute-done((f32[2,128,128]{2,1,0:T(8,128)S(1)}, f32[2,128,128]{2,1,0:T(8,128)S(1)}, u32[]{:S(2)}, u32[]{:S(2)}) %collective-permute-start.11) | collective-permute-done | bytes 131104 | tf_op jit(solution)/shard_map/ppermute | solution.py:297
  148.2 1.0 collective-permute-done.10.i1
  149.1 7.8 %all-to-all-done.5.cross_ref = f32[8,16,1024]{2,1,0:T(8,128)S(1)} async-done(((f32[8,16,1024]{2,1,0:T(8,128)}), f32[8,16,1024]{2,1,0:T(8,128)S(1)}, u32[]{:S(2)}, u32[]{:S(2)}) %all-to-all-start.5) | async-done | bytes 524320 | tf_op jit(solution)/shard_map/all_to_all | solution.py:391
  156.9 1.6 %solve.1 = f32[8,16,128]{2,1,0:T(8,128)} custom-call(s32[1]{0:T(128)} %bitcast.col_ref.r_0_, f32[8,16,1024]{2,1,0:T(8,128)S(1)} %all-to-all-done.5.cross_ref, f32[2,128,128]{2,1,0:T(8,128)S(1)} %factor.1.i0, f32[2,128,128]{2,1,0:T(8,128)S(1)} %collective-permute-done.10.i1, f32[2,128,128]{2,1,0:T(8,128)S(1)} %collective-permute-done.11.i2, ...), custom_call_target="tpu_custom_call" | custom-call | flops 1048576 | bytes 1048576 | tf_op jit(solution)/shard_map/solve/pallas_call | solution.py:393
  (13 shorter events, 0.0 us)
Async XLA Ops:
  0.0 25.6 %copy-start = (bf16[1024,1024]{1,0:T(8,128)(2,1)S(1)}, bf16[1024,1024]{1,0:T(8,128)(2,1)}, u32[]{:S(2)}) copy-start(bf16[1024,1024]{1,0:T(8,128)(2,1)} %child_ref.3) | copy-start | bytes 6291460
  0.0 5.0 %copy-start.5 = (s32[1024,1]{0,1:T(1,128)S(1)}, s32[1024,1]{0,1:T(1,128)}, u32[]{:S(2)}) copy-start(s32[1024,1]{0,1:T(1,128)} %param.9) | copy-start | bytes 12292
  0.0 10.2 %copy-start.6 = (s32[16]{0:T(128)S(1)}, s32[16]{0:T(128)}, u32[]{:S(2)}) copy-start(s32[16]{0:T(128)} %r_1_.3) | copy-start | bytes 196
  0.0 10.2 %copy-start.4 = (s32[1024]{0:T(1024)S(1)}, s32[1024]{0:T(1024)}, u32[]{:S(2)}) copy-start(s32[1024]{0:T(1024)} %param.10) | copy-start | bytes 12292
  2.4 7.8 %collective-permute-start = (bf16[64,1024]{1,0:T(8,128)(2,1)}, bf16[64,1024]{1,0:T(8,128)(2,1)S(1)}, u32[]{:S(2)}, u32[]{:S(2)}) collective-permute-start(bf16[64,1024]{1,0:T(8,128)(2,1)} %get-tuple-element.26), channel_id=1, source_target_pairs={{0,1},{4,5},{8,9},{12,13},{16,17},{20,21},{24,25},{28,29},{32,33},... | collective-permute-start | bytes 393224 | tf_op jit(solution)/shard_map/ppermute | solution.py:316
  3.7 6.6 %collective-permute-start.1 = (bf16[64,1024]{1,0:T(8,128)(2,1)}, bf16[64,1024]{1,0:T(8,128)(2,1)S(1)}, u32[]{:S(2)}, u32[]{:S(2)}) collective-permute-start(bf16[64,1024]{1,0:T(8,128)(2,1)} %get-tuple-element.27), channel_id=1, source_target_pairs={{0,2},{4,6},{8,10},{12,14},{16,18},{20,22},{24,26},{28,30},{32,34}... | collective-permute-start | bytes 393224 | tf_op jit(solution)/shard_map/ppermute | solution.py:316
  4.3 5.9 %collective-permute-start.2 = (bf16[64,1024]{1,0:T(8,128)(2,1)}, bf16[64,1024]{1,0:T(8,128)(2,1)S(1)}, u32[]{:S(2)}, u32[]{:S(2)}) collective-permute-start(bf16[64,1024]{1,0:T(8,128)(2,1)} %get-tuple-element.28), channel_id=1, source_target_pairs={{0,3},{4,7},{8,11},{12,15},{16,19},{20,23},{24,27},{28,31},{32,35}... | collective-permute-start | bytes 393224 | tf_op jit(solution)/shard_map/ppermute | solution.py:316
  10.2 0.9 copy-start.2
  13.6 24.8 %all-to-all-start = ((bf16[64,16,128]{2,1,0:T(8,128)(2,1)}), bf16[64,16,128]{2,1,0:T(8,128)(2,1)S(1)}, u32[]{:S(2)}, u32[]{:S(2)}) async-start(bf16[64,16,128]{2,1,0:T(8,128)(2,1)} %pack.1), calls=%async_computation | async-start | bytes 524288 | tf_op jit(solution)/shard_map/all_to_all | solution.py:331
  25.6 1.6 %copy-start.1 = (bf16[8,128,1024]{2,1,0:T(8,128)(2,1)S(1)}, bf16[8,128,1024]{2,1,0:T(8,128)(2,1)}, u32[]{:S(2)}) copy-start(bf16[8,128,1024]{2,1,0:T(8,128)(2,1)} %front_ref.3) | copy-start | bytes 6291460
  27.2 11.3 %copy-start.3 = (bf16[64,1024]{1,0:T(8,128)(2,1)S(1)}, bf16[64,1024]{1,0:T(8,128)(2,1)}, u32[]{:S(2)}) copy-start(bf16[64,1024]{1,0:T(8,128)(2,1)} %get-tuple-element.25.p0) | copy-start | bytes 393220
  27.2 51.8 %copy-start.7 = (s32[1,8]{1,0:T(1,128)S(1)}, s32[1,8]{1,0:T(1,128)}, u32[]{:S(2)}) copy-start(s32[1,8]{1,0:T(1,128)} %r_2_.3) | copy-start | bytes 100
  29.4 1.4 copy-start.8
  30.8 1.3 copy-start.10
  41.8 16.0 %all-to-all-start.1 = ((bf16[64,8,128]{2,1,0:T(8,128)(2,1)}), bf16[64,8,128]{2,1,0:T(8,128)(2,1)S(1)}, u32[]{:S(2)}, u32[]{:S(2)}) async-start(bf16[64,8,128]{2,1,0:T(8,128)(2,1)} %get-tuple-element.34), calls=%async_computation.1 | async-start | bytes 262144 | tf_op jit(solution)/shard_map/all_to_all | solution.py:340
  46.8 7.8 %collective-permute-start.5 = (bf16[32,1024]{1,0:T(8,128)(2,1)S(1)}, bf16[32,1024]{1,0:T(8,128)(2,1)S(1)}, u32[]{:S(2)}, u32[]{:S(2)}) collective-permute-start(bf16[32,1024]{1,0:T(8,128)(2,1)S(1)} %get-tuple-element.33.a0.r_4_), channel_id=1, source_target_pairs={{0,3},{1,0},{2,1},{3,2},{4,7},{5,4},{6,5},{7,6},{8,11},{9,8},{10,9... | collective-permute-start | bytes 196616 | tf_op jit(solution)/shard_map/ppermute | solution.py:297
  49.6 6.1 %collective-permute-start.4 = (bf16[32,1024]{1,0:T(8,128)(2,1)S(1)}, bf16[32,1024]{1,0:T(8,128)(2,1)S(1)}, u32[]{:S(2)}, u32[]{:S(2)}) collective-permute-start(bf16[32,1024]{1,0:T(8,128)(2,1)S(1)} %get-tuple-element.33.a0.r_4_), channel_id=1, source_target_pairs={{0,2},{1,3},{2,0},{3,1},{4,6},{5,7},{6,4},{7,5},{8,10},{9,11},{10,... | collective-permute-start | bytes 196616 | tf_op jit(solution)/shard_map/ppermute | solution.py:297
  52.1 4.5 %collective-permute-start.3 = (bf16[32,1024]{1,0:T(8,128)(2,1)S(1)}, bf16[32,1024]{1,0:T(8,128)(2,1)S(1)}, u32[]{:S(2)}, u32[]{:S(2)}) collective-permute-start(bf16[32,1024]{1,0:T(8,128)(2,1)S(1)} %get-tuple-element.33.a0.r_4_), channel_id=1, source_target_pairs={{0,1},{1,2},{2,3},{3,0},{4,5},{5,6},{6,7},{7,4},{8,9},{9,10},{10,1... | collective-permute-start | bytes 196616 | tf_op jit(solution)/shard_map/ppermute | solution.py:297
  57.8 21.0 %all-to-all-start.2 = ((f32[64,4,128]{2,1,0:T(4,128)}), f32[64,4,128]{2,1,0:T(4,128)S(1)}, u32[]{:S(2)}, u32[]{:S(2)}) async-start(f32[64,4,128]{2,1,0:T(4,128)} %bitcast.4), calls=%async_computation.2 | async-start | bytes 262144 | tf_op jit(solution)/shard_map/all_to_all | solution.py:349
  68.7 10.2 %collective-permute-start.8 = (bf16[32,1024]{1,0:T(8,128)(2,1)S(1)}, bf16[32,1024]{1,0:T(8,128)(2,1)S(1)}, u32[]{:S(2)}, u32[]{:S(2)}) collective-permute-start(bf16[32,1024]{1,0:T(8,128)(2,1)S(1)} %pick.1.r_8_), channel_id=1, source_target_pairs={{0,3},{1,0},{2,1},{3,2},{4,7},{5,4},{6,5},{7,6},{8,11},{9,8},{10,9... | collective-permute-start | bytes 196616 | tf_op jit(solution)/shard_map/ppermute | solution.py:297
  71.9 7.1 %collective-permute-start.7 = (bf16[32,1024]{1,0:T(8,128)(2,1)S(1)}, bf16[32,1024]{1,0:T(8,128)(2,1)S(1)}, u32[]{:S(2)}, u32[]{:S(2)}) collective-permute-start(bf16[32,1024]{1,0:T(8,128)(2,1)S(1)} %pick.1.r_8_), channel_id=1, source_target_pairs={{0,2},{1,3},{2,0},{3,1},{4,6},{5,7},{6,4},{7,5},{8,10},{9,11},{10,... | collective-permute-start | bytes 196616 | tf_op jit(solution)/shard_map/ppermute | solution.py:297
  72.6 6.3 %collective-permute-start.6 = (bf16[32,1024]{1,0:T(8,128)(2,1)S(1)}, bf16[32,1024]{1,0:T(8,128)(2,1)S(1)}, u32[]{:S(2)}, u32[]{:S(2)}) collective-permute-start(bf16[32,1024]{1,0:T(8,128)(2,1)S(1)} %pick.1.r_8_), channel_id=1, source_target_pairs={{0,1},{1,2},{2,3},{3,0},{4,5},{5,6},{6,7},{7,4},{8,9},{9,10},{10,1... | collective-permute-start | bytes 196616 | tf_op jit(solution)/shard_map/ppermute | solution.py:297
  78.9 14.9 %copy-start.9 = (bf16[4,8,16,2048]{3,2,1,0:T(8,128)(2,1)S(1)}, bf16[4,8,16,2048]{3,2,1,0:T(8,128)(2,1)}, u32[]{:S(2)}) copy-start(bf16[4,8,16,2048]{3,2,1,0:T(8,128)(2,1)} %copy-done.8) | copy-start | bytes 6291460
  79.0 1.7 %copy-start.11 = (bf16[4,8,16,2048]{3,2,1,0:T(8,128)(2,1)S(1)}, bf16[4,8,16,2048]{3,2,1,0:T(8,128)(2,1)}, u32[]{:S(2)}) copy-start(bf16[4,8,16,2048]{3,2,1,0:T(8,128)(2,1)} %copy-done.10) | copy-start | bytes 6291460
  84.2 11.8 %collective-permute-start.9 = (f32[512,1024]{1,0:T(8,128)}, f32[512,1024]{1,0:T(8,128)}, u32[]{:S(2)}, u32[]{:S(2)}) collective-permute-start(f32[512,1024]{1,0:T(8,128)} %cross0.1), channel_id=1, source_target_pairs={{0,4},{4,0},{8,12},{12,8},{16,20},{20,16},{24,28},{28,24},{32,36},... | collective-permute-start | bytes 6291464 | tf_op jit(solution)/shard_map/ppermute | solution.py:379
  85.0 19.9 %all-to-all-start.4 = ((f32[64,4,128]{2,1,0:T(4,128)}), f32[64,4,128]{2,1,0:T(4,128)S(1)}, u32[]{:S(2)}, u32[]{:S(2)}) async-start(f32[64,4,128]{2,1,0:T(4,128)} %broadcast_in_dim.14), calls=%async_computation.4 | async-start | bytes 262144 | tf_op jit(solution)/shard_map/all_to_all | solution.py:356
  104.9 30.5 %all-to-all-start.3 = ((f32[4,128,1024]{2,1,0:T(8,128)}), f32[4,128,1024]{2,1,0:T(8,128)S(1)}, u32[]{:S(2)}, u32[]{:S(2)}) async-start(f32[4,128,1024]{2,1,0:T(8,128)} %bitcast.5), calls=%async_computation.3 | async-start | bytes 4194304 | tf_op jit(solution)/shard_map/all_to_all | solution.py:387
  136.3 20.6 %all-to-all-start.5 = ((f32[8,16,1024]{2,1,0:T(8,128)}), f32[8,16,1024]{2,1,0:T(8,128)S(1)}, u32[]{:S(2)}, u32[]{:S(2)}) async-start(f32[8,16,1024]{2,1,0:T(8,128)} %bitcast.7), calls=%async_computation.5 | async-start | bytes 1048576 | tf_op jit(solution)/shard_map/all_to_all | solution.py:391
  139.8 5.5 %collective-permute-start.12 = (f32[2,128,128]{2,1,0:T(8,128)S(1)}, f32[2,128,128]{2,1,0:T(8,128)S(1)}, u32[]{:S(2)}, u32[]{:S(2)}) collective-permute-start(f32[2,128,128]{2,1,0:T(8,128)S(1)} %factor.1.i0), channel_id=1, source_target_pairs={{0,3},{1,0},{2,1},{3,2},{4,7},{5,4},{6,5},{7,6},{8,11},{9,8},{10,9... | collective-permute-start | bytes 393224 | tf_op jit(solution)/shard_map/ppermute | solution.py:297
  141.7 6.5 %collective-permute-start.11 = (f32[2,128,128]{2,1,0:T(8,128)S(1)}, f32[2,128,128]{2,1,0:T(8,128)S(1)}, u32[]{:S(2)}, u32[]{:S(2)}) collective-permute-start(f32[2,128,128]{2,1,0:T(8,128)S(1)} %factor.1.i0), channel_id=1, source_target_pairs={{0,2},{1,3},{2,0},{3,1},{4,6},{5,7},{6,4},{7,5},{8,10},{9,11},{10,... | collective-permute-start | bytes 393224 | tf_op jit(solution)/shard_map/ppermute | solution.py:297
  142.2 7.0 %collective-permute-start.10 = (f32[2,128,128]{2,1,0:T(8,128)S(1)}, f32[2,128,128]{2,1,0:T(8,128)S(1)}, u32[]{:S(2)}, u32[]{:S(2)}) collective-permute-start(f32[2,128,128]{2,1,0:T(8,128)S(1)} %factor.1.i0), channel_id=1, source_target_pairs={{0,1},{1,2},{2,3},{3,0},{4,5},{5,6},{6,7},{7,4},{8,9},{9,10},{10,1... | collective-permute-start | bytes 393224 | tf_op jit(solution)/shard_map/ppermute | solution.py:297
